TPU v7x, 32 devices: a whole 2x2x4 slice. The times are simulated.
32 devices in a mesh: gx: 8 (over z, y), gy: 4 (over x, core).
Axes of the slice: x: 2, y: 2, z: 4, core: 2. Of those that a mesh axis runs over, the one named last changes fastest.
Arguments:
- spectra: bfloat16 [64, 128, 2048], P('gx', 'gy'), may hold values from -48 to 48
- resample_index: int32 [2048], replicated, may hold values from 0 to 2046
- resample_weight: float32 [2048], replicated, may hold values from 0 to 1
- disp_phase: float32 [2048], replicated, may hold values from -3.140625 to 3.140625
- surface_block: int32 [64, 128], P('gx', 'gy'), may hold values from 0 to 3
Outputs:
- enface: float32 [640, 64, 128], P(('gx', 'gy'))
All inputs are finite; a program needn't handle non-finite values.
Results may differ from a plain program's by a relative error of at most 0.003.
Values sent between devices are 32-bit elements; how exact they have to be, the bound alone decides.
No kernel may reach another device: no remote copies, remote signals or barrier semaphores. Data moves between devices by JAX's collectives and lax.ppermute only.
A program may use at most 64 MiB of HBM per device.

v0:
```python
import math

import jax
import jax.numpy as jnp
from jax import lax
from jax.sharding import PartitionSpec as P

BLOCK = 128
KEEP = 5


def dft_table(samples, block):
    depths = samples // 2
    blocks = depths // block
    rows = jnp.arange(samples, dtype=jnp.int32)
    cols = jnp.arange(depths, dtype=jnp.int32)
    turns = (rows[:, None] * cols[None, :] % samples).astype(jnp.float32)
    angle = 2.0 * math.pi / samples * turns
    cosine = jnp.cos(angle).astype(jnp.bfloat16).reshape(samples, blocks, block)
    sine = jnp.sin(angle).astype(jnp.bfloat16).reshape(samples, blocks, block)
    upper = jnp.concatenate([cosine, -sine], axis=2)
    lower = jnp.concatenate([sine, cosine], axis=2)
    return jnp.concatenate([upper, lower], axis=0)


def resample_matrix(samples, resample_index, resample_weight):
    source = jnp.arange(samples, dtype=jnp.int32)[:, None]
    left_hit = (source == resample_index[None, :]).astype(jnp.float32)
    right_hit = (source == resample_index[None, :] + 1).astype(jnp.float32)
    return left_hit * (1.0 - resample_weight)[None, :] + right_hit * resample_weight[None, :]


def phase_planes(lines, resample_index, resample_weight, disp_phase):
    matrix = resample_matrix(lines.shape[1], resample_index, resample_weight)
    resampled = jnp.dot(
        lines.astype(jnp.float32),
        matrix,
        precision=lax.Precision.HIGHEST,
        preferred_element_type=jnp.float32,
    )
    real_part = (resampled * jnp.cos(disp_phase)).astype(jnp.bfloat16)
    imag_part = (resampled * jnp.sin(disp_phase)).astype(jnp.bfloat16)
    return jnp.concatenate([real_part, imag_part], axis=1)


def select_blocks(power, surface):
    blocks = power.shape[1]
    wanted = surface[:, None] + jnp.arange(KEEP, dtype=jnp.int32)[None, :]
    chooser = wanted[:, :, None] == jnp.arange(blocks, dtype=jnp.int32)[None, None, :]
    chosen = jnp.where(chooser[:, :, :, None], power[:, None, :, :], 0.0)
    return jnp.sum(chosen, axis=2)


def on_device(spectra, resample_index, resample_weight, disp_phase, surface_block):
    across, along, samples = spectra.shape
    count = across * along
    blocks = samples // (2 * BLOCK)
    table = dft_table(samples, BLOCK)
    lines = spectra.reshape(count, samples)
    stacked = phase_planes(lines, resample_index, resample_weight, disp_phase)
    surface = surface_block.reshape(count)
    depth = jnp.dot(
        stacked, table.reshape(2 * samples, blocks * 2 * BLOCK), preferred_element_type=jnp.float32
    )
    depth = depth.reshape(count, blocks, 2, BLOCK)
    power = depth[:, :, 0] * depth[:, :, 0] + depth[:, :, 1] * depth[:, :, 1]
    kept = select_blocks(power, surface).reshape(count, KEEP * BLOCK)
    total = lax.psum(jnp.sum(kept), ("gx", "gy"))
    width_x = lax.axis_size("gx")
    width_y = lax.axis_size("gy")
    level = total / (count * KEEP * BLOCK * width_x * width_y) + 1e-06
    image = jnp.log1p(kept / level)
    slabs = jnp.transpose(image.reshape(across, along, KEEP * BLOCK), (2, 0, 1))
    moved = lax.all_to_all(
        slabs.reshape(KEEP * BLOCK, 1, across, along),
        ("gx", "gy"),
        split_axis=0,
        concat_axis=1,
        tiled=True,
    )
    rows_out = moved.shape[0]
    moved = moved.reshape(rows_out, width_x, width_y, across, along)
    placed = jnp.transpose(moved, (0, 1, 3, 2, 4))
    return placed.reshape(rows_out, width_x * across, width_y * along)


def solution(mesh):
    placed = (P("gx", "gy", None), P(), P(), P(), P("gx", "gy"))
    return jax.shard_map(
        on_device,
        mesh=mesh,
        in_specs=placed,
        out_specs=P(("gx", "gy"), None, None),
        check_vma=False,
    )
```

profile of v0, /device:TPU:0, one launch (start us, length us, event | category | flops | bytes accessed | tf_op | source)
XLA Modules:
  0.0 196.8 jit_solution(1341242404284046245)
XLA Ops:
  0.0 0.0 copy-start
  0.0 0.0 copy-start.1
  0.0 34.5 %sine_convert_fusion = (bf16[2048,8,128]{0,2,1:T(8,128)(2,1)S(1)}, bf16[2048,8,128]{0,2,1:T(8,128)(2,1)S(1)}) fusion(s32[8,128]{1,0:T(8,128)S(1)} %multiply_add_fusion), kind=kLoop, calls=%fused_computation.13 | loop fusion | flops 33554432 | bytes 8392704 | tf_op jit(solution)/shard_map/convert_element_type | solution.py:20
  34.5 32.3 %fusion.18 = bf16[2048,8,128]{0,2,1:T(8,128)(2,1)S(1)} fusion(s32[8,128]{1,0:T(8,128)S(1)} %multiply_add_fusion), kind=kLoop, calls=%fused_computation.31 | loop fusion | flops 37748736 | bytes 4198400 | tf_op jit(solution)/shard_map/neg | solution.py:21
  66.8 0.0 copy-done.1
  66.8 0.0 copy-done.3
  66.9 0.0 copy-done.2
  66.9 6.9 %maximum_maximum_fusion = bf16[4096,8,256]{0,2,1:T(8,128)(2,1)} fusion(bf16[2048,8,128]{0,2,1:T(8,128)(2,1)S(1)} %get-tuple-element.12, bf16[2048,8,128]{0,2,1:T(8,128)(2,1)S(1)} %get-tuple-element.11, bf16[2048,8,128]{0,2,1:T(8,128)(2,1)S(1)} %fusion.18), kind=kLoop, calls=%fused_computation | loop fusion | flops 67108864 | bytes 29360128 | tf_op jit(solution)/shard_map/concatenate | solution.py:23
  73.8 0.0 copy-done
  73.8 16.2 %fusion.19 = (bf16[256,2048]{0,1:T(8,128)(2,1)S(1)}, bf16[256,2048]{0,1:T(8,128)(2,1)S(1)}) fusion(f32[2048]{0:T(1024)S(1)} %get-tuple-element.9, f32[2048]{0:T(1024)S(1)} %get-tuple-element.10, bf16[256,2048]{1,0:T(8,128)(2,1)S(1)} %bitcast.25, f32[2048]{0:T(1024)S(1)} %copy-done.2, s32[2048]{0:T(1024)S(1)} %broadcast_add_fusion, ...), kind=kOutput, calls=%fused_computation.32 | convolution fusion | flops 12907970560 | bytes 3194880 | tf_op jit(solution)/shard_map/dot_general | solution.py:35
  90.0 0.0 copy-start.4
  90.1 8.6 %fusion.15 = f32[256,8,2,128]{3,0,2,1:T(8,128)S(1)} fusion(bf16[8,2,128,4096]{3,2,1,0:T(8,128)(2,1)} %bitcast.26, bf16[256,2048]{0,1:T(8,128)(2,1)S(1)} %get-tuple-element.8, bf16[256,2048]{0,1:T(8,128)(2,1)S(1)} %get-tuple-element.7), kind=kOutput, calls=%fused_computation.26 | convolution fusion | flops 4299161600 | bytes 20971520 | tf_op jit(solution)/shard_map/dot_general | solution.py:62
  98.7 0.1 fusion.22
  98.8 0.6 copy.22
  99.5 0.0 copy-done.4
  99.5 0.1 add.63
  99.5 0.1 iota_add_fusion
  99.6 0.3 iota_compare_fusion.4
  100.0 3.1 %select_reduce_fusion = (f32[]{:T(128)}, f32[256,5,128]{2,1,0:T(8,128)S(1)}) fusion(f32[256,8,128]{2,1,0:T(8,128)S(1)} %copy.22, pred[256,5,8]{2,1,0:T(8,128)(4,1)S(1)} %iota_compare_fusion.4), kind=kLoop, calls=%fused_computation.23 | loop fusion | flops 3768319 | bytes 1714180 | tf_op jit(solution)/shard_map/reduce_sum | solution.py:68
  103.1 42.2 %psum.7 = f32[]{:T(128)} all-reduce(f32[]{:T(128)} %get-tuple-element.5), channel_id=1, replica_groups=mesh['gx'=8,'gy'=4] {'gx','gy'}, use_global_device_ids=true, to_apply=%region_2.3 | all-reduce | flops 1 | bytes 8 | tf_op jit(solution)/shard_map/psum | solution.py:68
  145.9 0.3 divide_log-plus-one_fusion
  146.2 0.2 log1p.8
  146.4 2.1 %copy.23 = f32[640,1,8,32]{3,2,1,0:T(8,128)} copy(f32[640,1,8,32]{0,3,2,1:T(8,128)S(1)} %bitcast.30) | data formatting | bytes 1310720 | tf_op jit(solution)/shard_map/reshape | solution.py:75
  148.5 2.7 %reshape.98 = f32[32,1,5120]{2,1,0:T(1,128)S(1)} reshape(f32[640,1,8,32]{3,2,1,0:T(8,128)} %copy.23) | data formatting | bytes 1310720
  151.2 22.4 %all_to_all.15 = f32[32,1,5120]{2,1,0:T(1,128)S(1)} all-to-all(f32[32,1,5120]{2,1,0:T(1,128)S(1)} %reshape.98), channel_id=1, replica_groups=mesh['gx'=8,'gy'=4] {'gx','gy'}, dimensions={0} | all-to-all | bytes 1310720 | tf_op jit(solution)/shard_map/all_to_all | solution.py:74
  173.6 0.5 broadcast.80
  174.1 2.2 %reduce.2 = f32[32,5120]{1,0:T(8,128)S(1)} reduce(f32[32,1,5120]{2,1,0:T(1,128)S(1)} %all_to_all.15, f32[]{:T(128)} %broadcast.80), dimensions={1}, to_apply=%all_to_all.11.reduce_sub_computation | reduce | bytes 1310724 | tf_op jit(solution)/shard_map/all_to_all | solution.py:74
  176.3 2.4 %reshape.99 = f32[640,1,8,32]{3,2,1,0:T(8,128)} reshape(f32[32,5120]{1,0:T(8,128)S(1)} %reduce.2) | data formatting | bytes 1310720
  178.7 5.2 %copy.29 = f32[32,20,1,8,32]{1,0,4,3,2:T(8,128)} copy(f32[32,20,1,8,32]{4,3,1,0,2:T(8,128)} %bitcast.28) | data formatting | bytes 1310720 | tf_op jit(solution)/shard_map/all_to_all | solution.py:74
  184.0 5.5 %copy.25 = f32[20,32,1,8,32]{4,3,1,0,2:T(8,128)} copy(f32[20,32,1,8,32]{0,1,4,3,2:T(8,128)} %bitcast.27) | data formatting | bytes 1310720 | tf_op jit(solution)/shard_map/all_to_all | solution.py:74
  189.4 4.1 %copy.26 = f32[20,8,8,4,32]{4,3,2,1,0:T(4,128)} copy(f32[20,8,8,4,32]{4,2,3,1,0:T(8,128)} %bitcast.29) | data formatting | bytes 1310720 | tf_op jit(solution)/shard_map/transpose | solution.py:83
  193.5 3.3 %reshape.96 = f32[20,64,128]{2,1,0:T(8,128)} reshape(f32[20,8,8,4,32]{4,3,2,1,0:T(4,128)} %copy.26) | data formatting | bytes 1310720 | tf_op jit(solution)/shard_map/reshape | solution.py:84
  (6 shorter events, 0.1 us)
Async XLA Ops:
  0.0 73.8 %copy-start = (bf16[8,32,2048]{2,1,0:T(8,128)(2,1)S(1)}, bf16[8,32,2048]{2,1,0:T(8,128)(2,1)}, u32[]{:S(2)}) copy-start(bf16[8,32,2048]{2,1,0:T(8,128)(2,1)} %param.5) | copy-start | bytes 3145732
  0.0 66.8 %copy-start.1 = (f32[2048]{0:T(1024)S(1)}, f32[2048]{0:T(1024)}, u32[]{:S(2)}) copy-start(f32[2048]{0:T(1024)} %param.8) | copy-start | bytes 24580
  0.0 66.8 %copy-start.3 = (s32[2048]{0:T(1024)S(1)}, s32[2048]{0:T(1024)}, u32[]{:S(2)}) copy-start(s32[2048]{0:T(1024)} %param.6) | copy-start | bytes 24580
  0.0 66.9 %copy-start.2 = (f32[2048]{0:T(1024)S(1)}, f32[2048]{0:T(1024)}, u32[]{:S(2)}) copy-start(f32[2048]{0:T(1024)} %param.7) | copy-start | bytes 24580
  90.0 9.4 %copy-start.4 = (s32[8,32]{1,0:T(8,128)S(1)}, s32[8,32]{1,0:T(8,128)}, u32[]{:S(2)}) copy-start(s32[8,32]{1,0:T(8,128)} %param.9) | copy-start | bytes 3076
where the time goes:
time: 197 us
  other arithmetic  79.9 us (41%)
  blocking collectives  64.6 us (33%)
  local copies, waits for them, and re-layouts  26.7 us (14%)
  matrix products  24.9 us (13%)
    psum x1, blocking collectives, on_device(): total = lax.psum(jnp.sum(kept), ('gx', 'gy'))  42.2 us
    convert_element_type x1, other arithmetic, dft_table(): sine = jnp.sin(angle).astype(jnp.bfloat16).reshape(samples, blocks, block)  34.5 us
    neg x1, other arithmetic, dft_table(): upper = jnp.concatenate([cosine, -sine], axis=2)  32.3 us
    all_to_all x1, blocking collectives, on_device(): lax.all_to_all(slabs.reshape(KEEP * BLOCK, 1, across, along), ('gx', 'gy'...  22.4 us
    dot_general x1, matrix products, phase_planes(): jnp.dot(lines.astype(jnp.float32), matrix, precision=lax.Precision.HIGHES...  16.2 us
    all_to_all x3, local copies, waits for them, and re-layouts, on_device(): lax.all_to_all(slabs.reshape(KEEP * BLOCK, 1, across, along), ('gx', 'gy'...  11.2 us
    dot_general x1, matrix products, on_device(): jnp.dot(stacked, table.reshape(2 * samples, blocks * 2 * BLOCK), preferre...  8.65 us
    concatenate x1, other arithmetic, dft_table(): return jnp.concatenate([upper, lower], axis=0)  6.93 us

commit v1 on v0

v1 whole, which is shorter than its diff:
```python
import functools
import math

import jax
import jax.numpy as jnp
from jax import lax
from jax.experimental import pallas as pl
from jax.experimental.pallas import tpu as pltpu
from jax.sharding import PartitionSpec as P

BLOCK = 128
KEEP = 5
LANES = 128
RADIX = 4
WINDOW = 512
JBLOCK = 256
NT = (((1,), (1,)), ((), ()))


def unit_circle(turns, samples):
    x = (turns - samples // 2).astype(jnp.float32) * (2.0 * math.pi / samples)
    s = x * x
    cosine = jnp.full_like(x, 1.0 / math.factorial(18))
    sine = jnp.full_like(x, 1.0 / math.factorial(19))
    for k in range(8, -1, -1):
        cosine = 1.0 / math.factorial(2 * k) - s * cosine
        sine = 1.0 / math.factorial(2 * k + 1) - s * sine
    return -cosine, -sine * x


def local_kernel(
    spec_ref, idx_ref, w_ref, cos_ref, sin_ref, surf_ref, out_ref,
    table, res, fold, flat, *, devices, rows, message,
):
    count, samples = spec_ref.shape
    short = samples // RADIX
    depths = samples // 2
    terms = depths // RADIX
    per_block = BLOCK // RADIX
    blocks = depths // BLOCK

    sub = lax.broadcasted_iota(jnp.int32, (8, short), 0)
    lane = lax.broadcasted_iota(jnp.int32, (8, short), 1)
    mask = samples - 1
    bases = [
        unit_circle(((RADIX * sub + q) * lane) & mask, samples) for q in range(RADIX)
    ]
    for g8 in range(terms // 64):
        rot_c, rot_s = unit_circle((8 * RADIX * (8 * g8 + sub) * lane) & mask, samples)
        for k in range(0, 8, 2):
            for q in range(RADIX):
                bc, bs = bases[q]
                both = []
                for t in (k, k + 1):
                    rc, rs = rot_c[t : t + 1], rot_s[t : t + 1]
                    both.append((bc * rc - bs * rs, bs * rc + bc * rs))
                row = (8 * g8 + k) * 8
                table[q, row : row + 16, :short] = jnp.concatenate(
                    [both[0][0], both[1][0]], axis=0
                ).astype(jnp.bfloat16)
                table[q, row : row + 16, short:] = jnp.concatenate(
                    [both[0][1], both[1][1]], axis=0
                ).astype(jnp.bfloat16)

    def gathered(j0, k0):
        cols = pl.ds(j0, JBLOCK)
        source = lax.broadcasted_iota(jnp.int32, (WINDOW, JBLOCK), 0) + k0
        left_of = idx_ref[:, cols]
        lhs = spec_ref[:, pl.ds(k0, WINDOW)]
        pick_left = (source == left_of).astype(jnp.float32).astype(jnp.bfloat16)
        pick_right = (source == left_of + 1).astype(jnp.float32).astype(jnp.bfloat16)
        left = jnp.dot(lhs, pick_left, preferred_element_type=jnp.float32)
        right = jnp.dot(lhs, pick_right, preferred_element_type=jnp.float32)
        w = w_ref[:, cols]
        return (1.0 - w) * left + w * right

    starts, ends = [], []
    for b in range(samples // JBLOCK):
        here = idx_ref[:, b * JBLOCK : (b + 1) * JBLOCK]
        low = jnp.min(here)
        k0 = jnp.minimum((low // LANES) * LANES, samples - WINDOW)
        starts.append(pl.multiple_of(k0, LANES))
        ends.append(jnp.max(here) + 2)
    for b, k0 in enumerate(starts):
        res[:, b * JBLOCK : (b + 1) * JBLOCK] = gathered(b * JBLOCK, k0)

    for b in range(samples // JBLOCK):
        first = starts[b] + WINDOW

        @pl.when(first < ends[b])
        def _():
            def step(i, carry):
                k = pl.multiple_of(first + i * LANES, LANES)
                j0 = b * JBLOCK
                source = lax.broadcasted_iota(jnp.int32, (LANES, JBLOCK), 0) + k
                cols = pl.ds(j0, JBLOCK)
                left_of = idx_ref[:, cols]
                lhs = spec_ref[:, pl.ds(k, LANES)]
                pl_ = (source == left_of).astype(jnp.float32).astype(jnp.bfloat16)
                pr_ = (source == left_of + 1).astype(jnp.float32).astype(jnp.bfloat16)
                left = jnp.dot(lhs, pl_, preferred_element_type=jnp.float32)
                right = jnp.dot(lhs, pr_, preferred_element_type=jnp.float32)
                w = w_ref[:, cols]
                res[:, cols] = res[:, cols] + ((1.0 - w) * left + w * right)
                return carry

            lax.fori_loop(0, (ends[b] - first + LANES - 1) // LANES, step, 0)

    for j in range(0, short, LANES):
        re, im = [], []
        for p in range(RADIX):
            cols = slice(p * short + j, p * short + j + LANES)
            r = res[:, cols]
            re.append((r * cos_ref[:, cols]).astype(jnp.bfloat16).astype(jnp.float32))
            im.append((r * sin_ref[:, cols]).astype(jnp.bfloat16).astype(jnp.float32))
        ar, ai = re[0] + re[2], im[0] + im[2]
        br, bi = re[0] - re[2], im[0] - im[2]
        cr, ci = re[1] + re[3], im[1] + im[3]
        dr, di = re[1] - re[3], im[1] - im[3]
        folded = [
            (ar + cr, ai + ci),
            (br + di, bi - dr),
            (ar - cr, ai - ci),
            (br - di, bi + dr),
        ]
        for q, (yr, yi) in enumerate(folded):
            yr, yi = yr.astype(jnp.bfloat16), yi.astype(jnp.bfloat16)
            fold[q, :count, j : j + LANES] = yr
            fold[q, :count, short + j : short + j + LANES] = yi
            fold[q, count:, j : j + LANES] = yi
            fold[q, count:, short + j : short + j + LANES] = -yr

    surface = surf_ref[...]
    total = jnp.zeros((8, LANES), jnp.float32)
    chosen = [surface == s for s in range(1, blocks - KEEP + 1)]
    for q in range(RADIX):
        depth = lax.dot_general(
            table[q], fold[q], NT, preferred_element_type=jnp.float32
        )
        re, im = depth[:, :count], depth[:, count:]
        power = re * re + im * im
        for k in range(KEEP):
            kept = power[k * per_block : (k + 1) * per_block]
            for s, hit in enumerate(chosen, 1):
                there = power[(k + s) * per_block : (k + s + 1) * per_block]
                kept = jnp.where(hit, there, kept)
            for h in range(count // LANES):
                half = kept[:, h * LANES : (h + 1) * LANES]
                total = total + jnp.sum(half.reshape(per_block // 8, 8, LANES), axis=0)
                flat[h, pl.ds(k * BLOCK + q, per_block, stride=RADIX), :] = half

    partial = jnp.sum(total, axis=0, keepdims=True)
    halves = count // LANES
    for dest in range(devices):
        base = dest * message
        for h in range(halves):
            out_ref[base + h * rows : base + (h + 1) * rows, :] = flat[
                h, dest * rows : (dest + 1) * rows, :
            ]
        out_ref[base + halves * rows : base + halves * rows + 1, :] = partial


def place_kernel(
    in_ref, out_ref, *, width_x, width_y, rows, message, across, along, scale
):
    devices = width_x * width_y
    halves = across * along // LANES
    chunks = LANES // along
    height = width_x * across
    groups = width_y // chunks
    sums = in_ref[pl.ds(halves * rows, devices, stride=message), :]
    level = jnp.sum(sums) * scale + 1e-06
    lane = lax.broadcasted_iota(jnp.int32, (1, LANES), 1)
    for gx in range(width_x):
        for group in range(groups):
            for h in range(halves):
                for r0 in range(0, rows, 8):
                    size = min(8, rows - r0)
                    parts = []
                    for c in range(chunks):
                        src = gx * width_y + group * chunks + c
                        start = src * message + h * rows + r0
                        parts.append(in_ref[start : start + size, :])
                    bit = 1
                    while bit < chunks:
                        upper = (lane // along) & bit != 0
                        mixed = list(parts)
                        for c in range(chunks):
                            if c & bit:
                                continue
                            a, b = parts[c], parts[c | bit]
                            mixed[c] = jnp.where(
                                upper, pltpu.roll(b, bit * along, 1), a
                            )
                            mixed[c | bit] = jnp.where(
                                upper, b, pltpu.roll(a, LANES - bit * along, 1)
                            )
                        parts = mixed
                        bit *= 2
                    for a in range(chunks):
                        x = gx * across + h * chunks + a
                        at = ((r0 * height + x - x % 8) * groups + group * 8) + x % 8
                        out_ref[pl.ds(at, size, stride=height * groups), :] = jnp.log1p(
                            parts[a] / level
                        )


def on_device(spectra, resample_index, resample_weight, disp_phase, surface_block):
    across, along, samples = spectra.shape
    count = across * along
    width_x = lax.axis_size("gx")
    width_y = lax.axis_size("gy")
    devices = width_x * width_y
    rows = KEEP * BLOCK // devices
    halves = count // LANES
    message = halves * rows + 1
    short = samples // RADIX
    terms = samples // 2 // RADIX
    vmem = pl.BlockSpec(memory_space=pltpu.VMEM)
    row = lambda v: v.reshape(1, v.size)
    sent = pl.pallas_call(
        functools.partial(local_kernel, devices=devices, rows=rows, message=message),
        out_shape=jax.ShapeDtypeStruct((devices * message, LANES), jnp.float32),
        in_specs=[vmem] * 6,
        out_specs=vmem,
        scratch_shapes=[
            pltpu.VMEM((RADIX, terms, 2 * short), jnp.bfloat16),
            pltpu.VMEM((count, samples), jnp.float32),
            pltpu.VMEM((RADIX, 2 * count, 2 * short), jnp.bfloat16),
            pltpu.VMEM((halves, KEEP * BLOCK, LANES), jnp.float32),
        ],
        name="local",
    )(
        spectra.reshape(count, samples),
        row(resample_index),
        row(resample_weight),
        row(jnp.cos(disp_phase)),
        row(jnp.sin(disp_phase)),
        row(surface_block),
    )
    moved = lax.all_to_all(
        sent.reshape(devices, message, 1, LANES),
        ("gx", "gy"),
        split_axis=0,
        concat_axis=0,
        tiled=True,
    ).reshape(devices * message, LANES)
    height, width = width_x * across, width_y * along
    groups = width // LANES
    placed = pl.pallas_call(
        functools.partial(
            place_kernel,
            width_x=width_x,
            width_y=width_y,
            rows=rows,
            message=message,
            across=across,
            along=along,
            scale=1.0 / (count * KEEP * BLOCK * devices),
        ),
        out_shape=jax.ShapeDtypeStruct((rows * height * groups, LANES), jnp.float32),
        in_specs=[vmem],
        out_specs=vmem,
        name="place",
    )(moved)
    placed = placed.reshape(rows, height // 8, groups, 8, LANES)
    return jnp.transpose(placed, (0, 1, 3, 2, 4)).reshape(rows, height, width)


def solution(mesh):
    placed = (P("gx", "gy", None), P(), P(), P(), P("gx", "gy"))
    return jax.shard_map(
        on_device,
        mesh=mesh,
        in_specs=placed,
        out_specs=P(("gx", "gy"), None, None),
        check_vma=False,
    )
```

time: 197 us -> 39.9 us (0.20)
  other arithmetic: 79.9 us -> 0 us
  blocking collectives: 64.6 us -> 25.7 us
  matrix products: 24.9 us -> 0 us
  local copies, waits for them, and re-layouts: 26.7 us -> 2.65 us
  Pallas kernels: 0 us -> 11.2 us
    psum x1 -> x0, blocking collectives: 42.2 us -> none  [on_device(): total = lax.psum(jnp.sum(kept), ('gx', 'gy'))]
    convert_element_type x1 -> x0, other arithmetic: 34.5 us -> none  [dft_table(): sine = jnp.sin(angle).astype(jnp.bfloat16).reshape(samples, blocks, block)]
    neg x1 -> x0, other arithmetic: 32.3 us -> none  [dft_table(): upper = jnp.concatenate([cosine, -sine], axis=2)]
    dot_general x2 -> x0, matrix products: 24.9 us -> none  [the longest x1 16.2 us: phase_planes(): jnp.dot(lines.astype(jnp.float32), matrix, precision=lax.Precision.HIGHES...]
    all_to_all x3 -> x0, local copies, waits for them, and re-layouts: 11.2 us -> none  [on_device(): lax.all_to_all(slabs.reshape(KEEP * BLOCK, 1, across, along), ('gx', 'gy'...]
    pallas_call x0 -> x2, Pallas kernels: none -> 11.2 us  [the longest x1 6.58 us: on_device(): pl.pallas_call(functools.partial(local_kernel, devices=devices, rows=rows...]
    concatenate x1 -> x0, other arithmetic: 6.93 us -> none  [dft_table(): return jnp.concatenate([upper, lower], axis=0)]
    unnamed x12 -> x0, local copies, waits for them, and re-layouts: 5.11 us -> none
where the time goes in v1:
time: 39.9 us; the launch traced here: 39.6 us
  blocking collectives  25.7 us (64%)
  Pallas kernels  11.2 us (28%)
  local copies, waits for them, and re-layouts  2.65 us (7%)
    all_to_all x1, blocking collectives, on_device(): lax.all_to_all(sent.reshape(devices, message, 1, LANES), ('gx', 'gy'), sp...  25.7 us
    pallas_call x1, Pallas kernels, on_device(): pl.pallas_call(functools.partial(local_kernel, devices=devices, rows=rows...  6.58 us
    pallas_call x1, Pallas kernels, on_device(): pl.pallas_call(functools.partial(place_kernel, width_x=width_x, width_y=w...  4.62 us
    sin x1, local copies, waits for them, and re-layouts, on_device(): jnp.sin(disp_phase)  1.34 us
    reshape x1, local copies, waits for them, and re-layouts, on_device(): row = lambda v: v.reshape(1, v.size)  1.31 us

profile of v1, /device:TPU:0, one launch (start us, length us, event | category | flops | bytes accessed | tf_op | source)
XLA Modules:
  0.0 39.6 jit_solution(3503925511844160510)
XLA Ops:
  0.0 1.3 %reshape.29.surf_ref = s32[1,256]{1,0:T(1,128)} reshape(s32[8,32]{1,0:T(8,128)} %param.9) | data formatting | bytes 2048 | tf_op jit(solution)/shard_map/reshape | solution.py:220
  1.3 1.3 %fusion = (f32[2048]{0:T(1024)}, f32[2048]{0:T(1024)}) fusion(f32[2048]{0:T(1024)} %param.8), kind=kLoop, calls=%fused_computation | loop fusion | bytes 24576 | tf_op jit(solution)/shard_map/sin | solution.py:238
  2.7 6.6 %local.1 = f32[1312,128]{1,0:T(8,128)} custom-call(bf16[256,2048]{1,0:T(8,128)(2,1)} %bitcast.10, s32[1,2048]{1,0:T(1,128)} %bitcast.13, f32[1,2048]{1,0:T(1,128)} %bitcast.14, f32[1,2048]{1,0:T(1,128)} %bitcast.12, f32[1,2048]{1,0:T(1,128)} %bitcast.11, s32[1,256]{1,0:T(1,128)} %reshape.29.surf_ref), custom_call_target="tpu_custom_call" | custom-call | tf_op jit(solution)/shard_map/local/pallas_call | solution.py:221
  9.2 25.7 %all_to_all.5 = f32[32,41,1,128]{3,2,1,0:T(1,128)} all-to-all(f32[32,41,1,128]{3,2,1,0:T(1,128)} %bitcast.8), channel_id=1, replica_groups=mesh['gx'=8,'gy'=4] {'gx','gy'}, dimensions={0} | all-to-all | bytes 1343488 | tf_op jit(solution)/shard_map/all_to_all | solution.py:241
  35.0 4.6 %place.1 = f32[1280,128]{1,0:T(8,128)} custom-call(f32[1312,128]{1,0:T(8,128)} %bitcast.9), custom_call_target="tpu_custom_call" | custom-call | tf_op jit(solution)/shard_map/place/pallas_call | solution.py:250

commit v2 on v1

v2 whole, which is shorter than its diff:
```python
import functools
import math

import jax
import jax.numpy as jnp
from jax import lax
from jax.experimental import pallas as pl
from jax.experimental.pallas import tpu as pltpu
from jax.sharding import PartitionSpec as P

BLOCK = 128
KEEP = 5
LANES = 128
RADIX = 4
WINDOW = 256
HALF = LANES // 2
LIMIT = 63 << 20
NT = (((1,), (1,)), ((), ()))


def circle(x):
    s = x * x
    cosine = jnp.full_like(x, 1.0 / math.factorial(18))
    sine = jnp.full_like(x, 1.0 / math.factorial(19))
    for k in range(8, -1, -1):
        cosine = 1.0 / math.factorial(2 * k) - s * cosine
        sine = 1.0 / math.factorial(2 * k + 1) - s * sine
    return cosine, sine * x


def unit_circle(turns, samples):
    x = (turns - samples // 2).astype(jnp.float32) * (2.0 * math.pi / samples)
    cosine, sine = circle(x)
    return -cosine, -sine


def local_kernel(
    spec_hbm, idx_hbm, w_hbm, phase_hbm, surf_hbm, out_ref,
    table, spec, idx, weight, phase, surf, real, imag, fold, flat, starts, sems,
    *, devices, rows, message,
):
    count, samples = spec_hbm.shape
    short = samples // RADIX
    depths = samples // 2
    terms = depths // RADIX
    per_block = BLOCK // RADIX
    blocks = depths // BLOCK
    pieces = samples // LANES
    halves = count // LANES

    small = [
        pltpu.make_async_copy(idx_hbm, idx, sems.at[0]),
        pltpu.make_async_copy(w_hbm, weight, sems.at[1]),
        pltpu.make_async_copy(phase_hbm, phase, sems.at[2]),
        pltpu.make_async_copy(surf_hbm, surf, sems.at[3]),
    ]
    large = pltpu.make_async_copy(spec_hbm, spec.at[0], sems.at[4])
    for copy in small:
        copy.start()
    large.start()

    sub = lax.broadcasted_iota(jnp.int32, (8, short), 0)
    lane = lax.broadcasted_iota(jnp.int32, (8, short), 1)
    mask = samples - 1
    bases = [
        unit_circle(((RADIX * sub + q) * lane) & mask, samples) for q in range(RADIX)
    ]
    for g8 in range(terms // 64):
        rot_c, rot_s = unit_circle((8 * RADIX * (8 * g8 + sub) * lane) & mask, samples)
        for k in range(0, 8, 2):
            for q in range(RADIX):
                bc, bs = bases[q]
                both = []
                for t in (k, k + 1):
                    rc, rs = rot_c[t : t + 1], rot_s[t : t + 1]
                    both.append((bc * rc - bs * rs, bs * rc + bc * rs))
                row = (8 * g8 + k) * 8
                table[q, row : row + 16, :short] = jnp.concatenate(
                    [both[0][0], both[1][0]], axis=0
                ).astype(jnp.bfloat16)
                table[q, row : row + 16, short:] = jnp.concatenate(
                    [both[0][1], both[1][1]], axis=0
                ).astype(jnp.bfloat16)

    for copy in small:
        copy.wait()
    index = idx[...]
    low = jnp.min(index, axis=1, keepdims=True)
    first = jnp.minimum((low // HALF) * HALF, samples - WINDOW)
    high = jnp.max(index, axis=1, keepdims=True) + 2
    missed = jnp.max(high - first) > WINDOW
    steps = (high - first + (LANES - 1)) // LANES
    cos_phase, sin_phase = circle(phase[...])
    ws = weight[...]
    large.wait()
    spec[1, :, : samples - HALF] = spec[0, :, HALF:]
    spec[1, :, samples - HALF :] = jnp.zeros((count, HALF), spec.dtype)

    source = lax.broadcasted_iota(jnp.int32, (WINDOW, LANES), 0).astype(jnp.bfloat16)

    def pick(near):
        hits = []
        for k in range(2):
            want = jnp.clip(near + k, -1, WINDOW).astype(jnp.bfloat16)
            hits.append(jnp.where(source == want, jnp.bfloat16(1), jnp.bfloat16(0)))
        return jnp.concatenate(hits, axis=1)

    def finish(pair, w, c, s):
        r = (1.0 - w) * pair[:, :LANES] + w * pair[:, LANES:]
        return (r * c).astype(jnp.bfloat16), (r * s).astype(jnp.bfloat16)

    def window(k0):
        odd = (k0 // HALF) & 1
        at = pl.multiple_of(k0 - odd * HALF, LANES)
        return spec[odd, :, pl.ds(at, WINDOW)]

    for b in range(pieces):
        k0 = first[b, 0]
        row = slice(b, b + 1)
        near = index[row] - first[row]
        pair = jnp.dot(window(k0), pick(near), preferred_element_type=jnp.float32)
        real[b], imag[b] = finish(pair, ws[row], cos_phase[row], sin_phase[row])

    @pl.when(missed)
    def _():
        for b in range(pieces):
            starts[b] = first[b, 0]
            starts[pieces + b] = steps[b, 0]

        def redo(b, carry):
            @pl.when(starts[pieces + b] * LANES > WINDOW)
            def _():
                near = idx[pl.ds(b, 1), :]

                def step(i, pair):
                    k = starts[b] + i * LANES
                    odd = (k // HALF) & 1
                    at = pl.multiple_of(k - odd * HALF, LANES)
                    lines = spec[odd, :, pl.ds(at, LANES)]
                    hits = pick(near - k)[:LANES]
                    return pair + jnp.dot(
                        lines, hits, preferred_element_type=jnp.float32
                    )

                pair = lax.fori_loop(
                    0,
                    starts[pieces + b],
                    step,
                    jnp.zeros((count, 2 * LANES), jnp.float32),
                )
                c, s = circle(phase[pl.ds(b, 1), :])
                re, im = finish(pair, weight[pl.ds(b, 1), :], c, s)
                real[b] = re
                imag[b] = im

            return carry

        lax.fori_loop(0, pieces, redo, 0)

    lines_at = [surf[x : x + 1, :] for x in range(surf.shape[0])]
    per_half = LANES // surf.shape[1]
    quarter = pieces // RADIX
    total = jnp.zeros((8, LANES), jnp.float32)

    @pl.loop(0, count // 16)
    def _(chunk):
        top = pl.ds(pl.multiple_of(chunk * 16, 16), 16)
        bottom = pl.ds(pl.multiple_of(count + chunk * 16, 16), 16)
        for j in range(quarter):
            re, im = [], []
            for p in range(RADIX):
                re.append(real[p * quarter + j, top].astype(jnp.float32))
                im.append(imag[p * quarter + j, top].astype(jnp.float32))
            ar, ai = re[0] + re[2], im[0] + im[2]
            br, bi = re[0] - re[2], im[0] - im[2]
            cr, ci = re[1] + re[3], im[1] + im[3]
            dr, di = re[1] - re[3], im[1] - im[3]
            folded = [
                (ar + cr, ai + ci),
                (br + di, bi - dr),
                (ar - cr, ai - ci),
                (br - di, bi + dr),
            ]
            left = slice(j * LANES, (j + 1) * LANES)
            right = slice(short + j * LANES, short + (j + 1) * LANES)
            for q, (yr, yi) in enumerate(folded):
                yr, yi = yr.astype(jnp.bfloat16), yi.astype(jnp.bfloat16)
                fold[q, top, left] = yr
                fold[q, top, right] = yi
                fold[q, bottom, left] = yi
                fold[q, bottom, right] = -yr

    surface = [
        jnp.concatenate(lines_at[h * per_half : (h + 1) * per_half], axis=1)
        for h in range(halves)
    ]
    surface = jnp.concatenate(surface, axis=1)
    chosen = [surface == s for s in range(1, blocks - KEEP + 1)]
    for q in range(RADIX):
        depth = lax.dot_general(
            table[q], fold[q], NT, preferred_element_type=jnp.float32
        )
        re, im = depth[:, :count], depth[:, count:]
        power = re * re + im * im
        for k in range(KEEP):
            kept = power[k * per_block : (k + 1) * per_block]
            for s, hit in enumerate(chosen, 1):
                there = power[(k + s) * per_block : (k + s + 1) * per_block]
                kept = jnp.where(hit, there, kept)
            base = q * (KEEP * per_block) + k * per_block
            for h in range(halves):
                half = kept[:, h * LANES : (h + 1) * LANES]
                total = total + jnp.sum(half.reshape(per_block // 8, 8, LANES), axis=0)
                flat[h, base : base + per_block, :] = half
    for h in range(halves):
        for m in range(KEEP * per_block):
            four = flat[h, pl.ds(m, RADIX, stride=KEEP * per_block), :]
            r = RADIX * m
            while r < RADIX * (m + 1):
                dest = r // rows
                stop = min(RADIX * (m + 1), (dest + 1) * rows)
                at = dest * message + h * rows + r % rows
                out_ref[at : at + stop - r, :] = four[
                    r - RADIX * m : stop - RADIX * m
                ]
                r = stop

    partial = jnp.sum(total, axis=0, keepdims=True)
    for dest in range(devices):
        at = dest * message + halves * rows
        out_ref[at : at + 1, :] = partial


def place_kernel(
    in_ref, out_hbm, stage, sem, *, width_x, width_y, rows, message, across, along, scale
):
    devices = width_x * width_y
    halves = across * along // LANES
    chunks = LANES // along
    groups = width_y // chunks
    sums = in_ref[pl.ds(halves * rows, devices, stride=message), :]
    inverse = 1.0 / (jnp.sum(sums) * scale + 1e-06)
    lane = lax.broadcasted_iota(jnp.int32, (1, LANES), 1)
    copies = []
    for gx in range(width_x):
        for group in range(groups):
            for h in range(halves):
                for r0 in range(0, rows, 8):
                    size = min(8, rows - r0)
                    parts = []
                    for c in range(chunks):
                        src = gx * width_y + group * chunks + c
                        start = src * message + h * rows + r0
                        parts.append(
                            jnp.log(1.0 + in_ref[start : start + size, :] * inverse)
                        )
                    bit = 1
                    while bit < chunks:
                        upper = (lane // along) & bit != 0
                        mixed = list(parts)
                        for c in range(chunks):
                            if c & bit:
                                continue
                            a, b = parts[c], parts[c | bit]
                            if 2 * bit == chunks:
                                up = down = pltpu.roll(
                                    jnp.where(upper, a, b), LANES // 2, 1
                                )
                            else:
                                up = pltpu.roll(b, bit * along, 1)
                                down = pltpu.roll(a, LANES - bit * along, 1)
                            mixed[c] = jnp.where(upper, up, a)
                            mixed[c | bit] = jnp.where(upper, b, down)
                        parts = mixed
                        bit *= 2
                    for a in range(chunks):
                        at = (gx * across + h * chunks + a) * groups + group
                        stage[at, r0 : r0 + size, :] = parts[a]
                for a in range(chunks):
                    x = gx * across + h * chunks + a
                    copy = pltpu.make_async_copy(
                        stage.at[x * groups + group],
                        out_hbm.at[:, x // 8, group, x % 8],
                        sem.at[x * groups + group],
                    )
                    copy.start()
                    copies.append(copy)
    for copy in copies:
        copy.wait()


def on_device(spectra, resample_index, resample_weight, disp_phase, surface_block):
    across, along, samples = spectra.shape
    count = across * along
    width_x = lax.axis_size("gx")
    width_y = lax.axis_size("gy")
    devices = width_x * width_y
    rows = KEEP * BLOCK // devices
    halves = count // LANES
    message = halves * rows + 1
    short = samples // RADIX
    terms = samples // 2 // RADIX
    pieces = samples // LANES
    vmem = pl.BlockSpec(memory_space=pltpu.VMEM)
    hbm = pl.BlockSpec(memory_space=pltpu.HBM)
    sent = pl.pallas_call(
        functools.partial(local_kernel, devices=devices, rows=rows, message=message),
        out_shape=jax.ShapeDtypeStruct((devices * message, LANES), jnp.float32),
        in_specs=[hbm] * 5,
        out_specs=vmem,
        scratch_shapes=[
            pltpu.VMEM((RADIX, terms, 2 * short), jnp.bfloat16),
            pltpu.VMEM((2, count, samples), jnp.bfloat16),
            pltpu.VMEM((pieces, LANES), jnp.int32),
            pltpu.VMEM((pieces, LANES), jnp.float32),
            pltpu.VMEM((pieces, LANES), jnp.float32),
            pltpu.VMEM((across, along), jnp.int32),
            pltpu.VMEM((pieces, count, LANES), jnp.bfloat16),
            pltpu.VMEM((pieces, count, LANES), jnp.bfloat16),
            pltpu.VMEM((RADIX, 2 * count, 2 * short), jnp.bfloat16),
            pltpu.VMEM((halves, KEEP * BLOCK, LANES), jnp.float32),
            pltpu.SMEM((2 * pieces,), jnp.int32),
            pltpu.SemaphoreType.DMA((5,)),
        ],
        compiler_params=pltpu.CompilerParams(vmem_limit_bytes=LIMIT),
        name="local",
    )(
        spectra.reshape(count, samples),
        resample_index.reshape(pieces, LANES),
        resample_weight.reshape(pieces, LANES),
        disp_phase.reshape(pieces, LANES),
        surface_block,
    )
    moved = lax.all_to_all(
        sent.reshape(devices, message, 1, LANES),
        ("gx", "gy"),
        split_axis=0,
        concat_axis=0,
        tiled=True,
    ).reshape(devices * message, LANES)
    height, width = width_x * across, width_y * along
    groups = width // LANES
    placed = pl.pallas_call(
        functools.partial(
            place_kernel,
            width_x=width_x,
            width_y=width_y,
            rows=rows,
            message=message,
            across=across,
            along=along,
            scale=1.0 / (count * KEEP * BLOCK * devices),
        ),
        out_shape=jax.ShapeDtypeStruct(
            (rows, height // 8, groups, 8, LANES), jnp.float32
        ),
        in_specs=[vmem],
        out_specs=hbm,
        scratch_shapes=[
            pltpu.VMEM((height * groups, rows, LANES), jnp.float32),
            pltpu.SemaphoreType.DMA((height * groups,)),
        ],
        compiler_params=pltpu.CompilerParams(vmem_limit_bytes=8 << 20),
        name="place",
    )(moved)
    return jnp.transpose(placed, (0, 1, 3, 2, 4)).reshape(rows, height, width)


def solution(mesh):
    placed = (P("gx", "gy", None), P(), P(), P(), P("gx", "gy"))
    return jax.shard_map(
        on_device,
        mesh=mesh,
        in_specs=placed,
        out_specs=P(("gx", "gy"), None, None),
        check_vma=False,
    )
```

time: 39.9 us -> 33.8 us (0.85)
  Pallas kernels: 11.2 us -> 7.95 us
  local copies, waits for them, and re-layouts: 2.65 us -> 0 us
    pallas_call x1, Pallas kernels: 4.62 us -> 1.8 us  [on_device(): pl.pallas_call(functools.partial(place_kernel, width_x=width_x, width_y=w...]
    sin x1 -> x0, local copies, waits for them, and re-layouts: 1.34 us -> none  [on_device(): jnp.sin(disp_phase)]
    reshape x1 -> x0, local copies, waits for them, and re-layouts: 1.31 us -> none  [on_device(): row = lambda v: v.reshape(1, v.size)]
    pallas_call x1, Pallas kernels: 6.58 us -> 6.14 us  [on_device(): pl.pallas_call(functools.partial(local_kernel, devices=devices, rows=rows...]
where the time goes in v2:
time: 33.8 us; the launch traced here: 33.6 us
  blocking collectives  25.6 us (76%)
  Pallas kernels  7.95 us (24%)
    all_to_all x1, blocking collectives, on_device(): lax.all_to_all(sent.reshape(devices, message, 1, LANES), ('gx', 'gy'), sp...  25.6 us
    pallas_call x1, Pallas kernels, on_device(): pl.pallas_call(functools.partial(local_kernel, devices=devices, rows=rows...  6.14 us
    pallas_call x1, Pallas kernels, on_device(): pl.pallas_call(functools.partial(place_kernel, width_x=width_x, width_y=w...  1.8 us

profile of v2, /device:TPU:0, one launch (start us, length us, event | category | flops | bytes accessed | tf_op | source)
XLA Modules:
  0.0 33.6 jit_solution(15252763436281110090)
XLA Ops:
  0.0 6.1 %local.1 = f32[1312,128]{1,0:T(8,128)} custom-call(bf16[256,2048]{1,0:T(8,128)(2,1)} %bitcast.9, s32[16,128]{1,0:T(8,128)} %bitcast.10, f32[16,128]{1,0:T(8,128)} %bitcast.11, f32[16,128]{1,0:T(8,128)} %bitcast.12, s32[8,32]{1,0:T(8,128)} %surf_hbm.1), custom_call_target="tpu_custom_call" | custom-call | tf_op jit(solution)/shard_map/local/pallas_call | solution.py:306
  6.2 25.6 %all_to_all.5 = f32[32,41,1,128]{3,2,1,0:T(1,128)S(1)} all-to-all(f32[32,41,1,128]{3,2,1,0:T(1,128)} %bitcast.8), channel_id=1, replica_groups=mesh['gx'=8,'gy'=4] {'gx','gy'}, dimensions={0} | all-to-all | bytes 1343488 | tf_op jit(solution)/shard_map/all_to_all | solution.py:334
  31.8 1.8 %place.1 = f32[20,8,1,8,128]{4,3,2,1,0:T(8,128)} custom-call(f32[1312,128]{1,0:T(8,128)S(1)} %bitcast.7), custom_call_target="tpu_custom_call" | custom-call | tf_op jit(solution)/shard_map/place/pallas_call | solution.py:343

commit v3 on v2

v3 whole, which is shorter than its diff:
```python
import functools
import math

import jax
import jax.numpy as jnp
from jax import lax
from jax.experimental import pallas as pl
from jax.experimental.pallas import tpu as pltpu
from jax.sharding import PartitionSpec as P

BLOCK = 128
KEEP = 5
LANES = 128
RADIX = 4
WINDOW = 256
PAIR = 2
LIMIT = 63 << 20
NT = (((1,), (1,)), ((), ()))


def circle(x):
    s = x * x
    cosine = jnp.full_like(x, 1.0 / math.factorial(18))
    sine = jnp.full_like(x, 1.0 / math.factorial(19))
    for k in range(8, -1, -1):
        cosine = 1.0 / math.factorial(2 * k) - s * cosine
        sine = 1.0 / math.factorial(2 * k + 1) - s * sine
    return cosine, sine * x


def unit_circle(turns, samples):
    x = (turns - samples // 2).astype(jnp.float32) * (2.0 * math.pi / samples)
    cosine, sine = circle(x)
    return -cosine, -sine


def place_in_message(r, rows):
    if rows % RADIX:
        return r
    return (r % RADIX) * (rows // RADIX) + r // RADIX


def local_kernel(
    spec_hbm, idx_hbm, w_hbm, phase_hbm, surf_hbm, out_ref,
    table, spec, idx, weight, phase, surf, real, imag, fold, total, starts, sems,
    *, devices, rows, message,
):
    count, samples = spec_hbm.shape
    short = samples // RADIX
    depths = samples // 2
    terms = depths // RADIX
    per_block = BLOCK // RADIX
    blocks = depths // BLOCK
    pieces = samples // LANES
    quarter = pieces // RADIX
    halves = count // LANES

    small = [
        pltpu.make_async_copy(idx_hbm, idx, sems.at[0]),
        pltpu.make_async_copy(w_hbm, weight, sems.at[1]),
        pltpu.make_async_copy(phase_hbm, phase, sems.at[2]),
        pltpu.make_async_copy(surf_hbm, surf, sems.at[3]),
    ]
    large = pltpu.make_async_copy(spec_hbm, spec, sems.at[4])
    for copy in small:
        copy.start()
    large.start()

    sub = lax.broadcasted_iota(jnp.int32, (8, short), 0)
    lane = lax.broadcasted_iota(jnp.int32, (8, short), 1)
    mask = samples - 1
    bases = [
        unit_circle(((RADIX * sub + q) * lane) & mask, samples) for q in range(RADIX)
    ]
    for g8 in range(terms // 64):
        rot_c, rot_s = unit_circle((8 * RADIX * (8 * g8 + sub) * lane) & mask, samples)
        for k in range(0, 8, 2):
            for q in range(RADIX):
                bc, bs = bases[q]
                both = []
                for t in (k, k + 1):
                    rc, rs = rot_c[t : t + 1], rot_s[t : t + 1]
                    both.append((bc * rc - bs * rs, bs * rc + bc * rs))
                row = (8 * g8 + k) * 8
                table[q, row : row + 16, :short] = jnp.concatenate(
                    [both[0][0], both[1][0]], axis=0
                ).astype(jnp.bfloat16)
                table[q, row : row + 16, short:] = jnp.concatenate(
                    [both[0][1], both[1][1]], axis=0
                ).astype(jnp.bfloat16)
    total[...] = jnp.zeros_like(total)

    for copy in small:
        copy.wait()
    index = idx[...]
    low = jnp.min(index, axis=1, keepdims=True)
    first = jnp.minimum((low // LANES) * LANES, samples - WINDOW)
    high = jnp.max(index, axis=1, keepdims=True) + 2
    longest = jnp.max(high - first)
    steps = (high - first + (LANES - 1)) // LANES
    cos_phase, sin_phase = circle(phase[...])
    ws = weight[...]
    vs = 1.0 - ws
    near_all = index - first
    large.wait()

    source = lax.broadcasted_iota(jnp.int32, (WINDOW, LANES), 0).astype(jnp.bfloat16)

    def pick(near):
        hits = []
        for k in range(2):
            want = jnp.clip(near + k, -1, WINDOW).astype(jnp.bfloat16)
            hits.append(jnp.where(source == want, jnp.bfloat16(1), jnp.bfloat16(0)))
        return jnp.concatenate(hits, axis=1)

    def finish(pair, v, w, c, s):
        r = v * pair[:, :LANES] + w * pair[:, LANES:]
        return (r * c).astype(jnp.bfloat16), (r * s).astype(jnp.bfloat16)

    for b in range(pieces):
        row = slice(b, b + 1)
        lines = spec[:, pl.ds(pl.multiple_of(first[b, 0], LANES), WINDOW)]
        pair = jnp.dot(lines, pick(near_all[row]), preferred_element_type=jnp.float32)
        real[b], imag[b] = finish(pair, vs[row], ws[row], cos_phase[row], sin_phase[row])

    @pl.when(longest > WINDOW)
    def _():
        for b in range(pieces):
            starts[b] = first[b, 0]
            starts[pieces + b] = steps[b, 0]

        def redo(b, carry):
            @pl.when(starts[pieces + b] * LANES > WINDOW)
            def _():
                near = idx[pl.ds(b, 1), :]

                def step(i, pair):
                    k = pl.multiple_of(starts[b] + i * LANES, LANES)
                    hits = pick(near - k)[:LANES]
                    return pair + jnp.dot(
                        spec[:, pl.ds(k, LANES)],
                        hits,
                        preferred_element_type=jnp.float32,
                    )

                pair = lax.fori_loop(
                    0,
                    starts[pieces + b],
                    step,
                    jnp.zeros((count, 2 * LANES), jnp.float32),
                )
                c, s = circle(phase[pl.ds(b, 1), :])
                w = weight[pl.ds(b, 1), :]
                re, im = finish(pair, 1.0 - w, w, c, s)
                real[b] = re
                imag[b] = im

            return carry

        lax.fori_loop(0, pieces, redo, 0)

    def fold_lines(h, r0):
        at = pl.ds(pl.multiple_of(h * LANES + r0, 16), 16)
        top = pl.ds(pl.multiple_of(r0, 16), 16)
        bottom = pl.ds(pl.multiple_of(LANES + r0, 16), 16)
        for j in range(quarter):
            re, im = [], []
            for p in range(RADIX):
                re.append(real[p * quarter + j, at].astype(jnp.float32))
                im.append(imag[p * quarter + j, at].astype(jnp.float32))
            ar, ai = re[0] + re[2], im[0] + im[2]
            br, bi = re[0] - re[2], im[0] - im[2]
            cr, ci = re[1] + re[3], im[1] + im[3]
            dr, di = re[1] - re[3], im[1] - im[3]
            folded = [
                (ar + cr, ai + ci),
                (br + di, bi - dr),
                (ar - cr, ai - ci),
                (br - di, bi + dr),
            ]
            left = slice(j * LANES, (j + 1) * LANES)
            right = slice(short + j * LANES, short + (j + 1) * LANES)
            for q, (yr, yi) in enumerate(folded):
                yr, yi = yr.astype(jnp.bfloat16), yi.astype(jnp.bfloat16)
                fold[h, q, top, left] = yr
                fold[h, q, top, right] = yi
                fold[h, q, bottom, left] = yi
                fold[h, q, bottom, right] = -yr

    per_half = LANES // surf.shape[1]

    def transform(h, q):
        lines_at = range(h * per_half, (h + 1) * per_half)
        surface = jnp.concatenate([surf[x : x + 1, :] for x in lines_at], axis=1)
        chosen = [surface == s for s in range(1, blocks - KEEP + 1)]
        depth = lax.dot_general(
            table[q], fold[h, q], NT, preferred_element_type=jnp.float32
        )
        re, im = depth[:, :LANES], depth[:, LANES:]
        power = re * re + im * im
        for k in range(KEEP):
            kept = power[k * per_block : (k + 1) * per_block]
            for s, hit in enumerate(chosen, 1):
                there = power[(k + s) * per_block : (k + s + 1) * per_block]
                kept = jnp.where(hit, there, kept)
            total[...] += jnp.sum(kept.reshape(per_block // 8, 8, LANES), axis=0)
            places = []
            for m in range(per_block):
                r = (k * per_block + m) * RADIX + q
                inside = place_in_message(r % rows, rows)
                places.append((r // rows) * message + h * rows + inside)
            m = 0
            while m < per_block:
                stop = m + 1
                while stop % 8 and places[stop] == places[stop - 1] + 1:
                    stop += 1
                out_ref[places[m] : places[m] + stop - m, :] = kept[m:stop]
                m = stop

    @pl.loop(0, LANES // 32)
    def _(chunk):
        for part in range(2):
            fold_lines(0, chunk * 32 + part * 16)

    for h in range(halves):
        for q0 in range(0, RADIX, PAIR):

            @pl.when(longest > 0)
            def _():
                for q in range(q0, q0 + PAIR):
                    transform(h, q)
                if h + 1 < halves:
                    share = LANES * PAIR // RADIX
                    begin = q0 // PAIR * share
                    for r0 in range(begin, begin + share, 16):
                        fold_lines(h + 1, r0)

    partial = jnp.sum(total[...], axis=0, keepdims=True)
    for dest in range(devices):
        at = dest * message + halves * rows
        out_ref[at : at + 1, :] = partial


def swap_chunks(parts, along, lane):
    chunks = len(parts)
    bit = 1
    while bit < chunks:
        upper = (lane // along) & bit != 0
        mixed = list(parts)
        for c in range(chunks):
            if c & bit:
                continue
            a, b = parts[c], parts[c | bit]
            if 2 * bit == chunks:
                up = down = pltpu.roll(jnp.where(upper, a, b), LANES // 2, 1)
            else:
                up = pltpu.roll(b, bit * along, 1)
                down = pltpu.roll(a, LANES - bit * along, 1)
            mixed[c] = jnp.where(upper, up, a)
            mixed[c | bit] = jnp.where(upper, b, down)
        parts = mixed
        bit *= 2
    return parts


def place_kernel(
    in_ref, out_hbm, stage, sem, *, width_x, width_y, rows, message, across, along, scale
):
    devices = width_x * width_y
    halves = across * along // LANES
    chunks = LANES // along
    groups = width_y // chunks
    sums = in_ref[pl.ds(halves * rows, devices, stride=message), :]
    inverse = 1.0 / (jnp.sum(sums) * scale + 1e-06)
    lane = lax.broadcasted_iota(jnp.int32, (1, LANES), 1)
    outer, inner = stage.shape[2], stage.shape[4]

    for gx in range(width_x):
        for group in range(groups):
            at = gx * groups + group
            heads = [
                (gx * width_y + group * chunks + c) * message for c in range(chunks)
            ]
            for u in range(outer):
                if inner == RADIX:
                    blocks = [pl.ds(head + u, halves * inner, stride=outer) for head in heads]
                    blocks = [jnp.log(1.0 + in_ref[b, :] * inverse) for b in blocks]
                    blocks = swap_chunks(blocks, along, lane)
                    for a in range(chunks):
                        for h in range(halves):
                            stage[at, a, u, h] = blocks[a][h * inner : (h + 1) * inner]
                else:
                    for h in range(halves):
                        blocks = [pl.ds(head + h * rows + u * inner, inner) for head in heads]
                        blocks = [jnp.log(1.0 + in_ref[b, :] * inverse) for b in blocks]
                        blocks = swap_chunks(blocks, along, lane)
                        for a in range(chunks):
                            stage[at, a, u, h] = blocks[a]
            for h in range(halves):
                for a in range(chunks):
                    x = gx * across + h * chunks + a
                    pltpu.make_async_copy(
                        stage.at[at, a, :, h],
                        out_hbm.at[:, :, x // 8, group, x % 8],
                        sem,
                    ).start()
    pltpu.make_async_copy(stage, stage, sem).wait()


def on_device(spectra, resample_index, resample_weight, disp_phase, surface_block):
    across, along, samples = spectra.shape
    count = across * along
    width_x = lax.axis_size("gx")
    width_y = lax.axis_size("gy")
    devices = width_x * width_y
    rows = KEEP * BLOCK // devices
    halves = count // LANES
    message = halves * rows + 1
    short = samples // RADIX
    terms = samples // 2 // RADIX
    pieces = samples // LANES
    vmem = pl.BlockSpec(memory_space=pltpu.VMEM)
    hbm = pl.BlockSpec(memory_space=pltpu.HBM)
    sent = pl.pallas_call(
        functools.partial(local_kernel, devices=devices, rows=rows, message=message),
        out_shape=jax.ShapeDtypeStruct((devices * message, LANES), jnp.float32),
        in_specs=[hbm] * 5,
        out_specs=vmem,
        scratch_shapes=[
            pltpu.VMEM((RADIX, terms, 2 * short), jnp.bfloat16),
            pltpu.VMEM((count, samples), jnp.bfloat16),
            pltpu.VMEM((pieces, LANES), jnp.int32),
            pltpu.VMEM((pieces, LANES), jnp.float32),
            pltpu.VMEM((pieces, LANES), jnp.float32),
            pltpu.VMEM((across, along), jnp.int32),
            pltpu.VMEM((pieces, count, LANES), jnp.bfloat16),
            pltpu.VMEM((pieces, count, LANES), jnp.bfloat16),
            pltpu.VMEM((halves, RADIX, 2 * LANES, 2 * short), jnp.bfloat16),
            pltpu.VMEM((8, LANES), jnp.float32),
            pltpu.SMEM((2 * pieces,), jnp.int32),
            pltpu.SemaphoreType.DMA((5,)),
        ],
        compiler_params=pltpu.CompilerParams(vmem_limit_bytes=LIMIT),
        name="local",
    )(
        spectra.reshape(count, samples),
        resample_index.reshape(pieces, LANES),
        resample_weight.reshape(pieces, LANES),
        disp_phase.reshape(pieces, LANES),
        surface_block,
    )
    moved = lax.all_to_all(
        sent.reshape(devices, message, 1, LANES),
        ("gx", "gy"),
        split_axis=0,
        concat_axis=0,
        tiled=True,
    ).reshape(devices * message, LANES)
    height, width = width_x * across, width_y * along
    groups = width // LANES
    inner = rows if rows % RADIX else RADIX
    placed = pl.pallas_call(
        functools.partial(
            place_kernel,
            width_x=width_x,
            width_y=width_y,
            rows=rows,
            message=message,
            across=across,
            along=along,
            scale=1.0 / (count * KEEP * BLOCK * devices),
        ),
        out_shape=jax.ShapeDtypeStruct(
            (rows // inner, inner, height // 8, groups, 8, LANES), jnp.float32
        ),
        in_specs=[vmem],
        out_specs=hbm,
        scratch_shapes=[
            pltpu.VMEM(
                (width_x * groups, LANES // along, rows // inner, halves, inner, LANES),
                jnp.float32,
            ),
            pltpu.SemaphoreType.DMA,
        ],
        compiler_params=pltpu.CompilerParams(vmem_limit_bytes=8 << 20),
        name="place",
    )(moved)
    placed = placed.reshape(rows, height // 8, groups, 8, LANES)
    return jnp.transpose(placed, (0, 1, 3, 2, 4)).reshape(rows, height, width)


def solution(mesh):
    placed = (P("gx", "gy", None), P(), P(), P(), P("gx", "gy"))
    return jax.shard_map(
        on_device,
        mesh=mesh,
        in_specs=placed,
        out_specs=P(("gx", "gy"), None, None),
        check_vma=False,
    )
```

time: 33.8 us -> 33.5 us (level)
  Pallas kernels: 7.95 us -> 7.61 us
    pallas_call x1, Pallas kernels: 6.14 us -> 5.35 us  [on_device(): pl.pallas_call(functools.partial(local_kernel, devices=devices, rows=rows...]
    pallas_call x1, Pallas kernels: 1.8 us -> 2.25 us  [on_device(): pl.pallas_call(functools.partial(place_kernel, width_x=width_x, width_y=w...]
where the time goes in v3:
time: 33.5 us; the launch traced here: 33.2 us
  blocking collectives  25.6 us (76%)
  Pallas kernels  7.61 us (23%)
    all_to_all x1, blocking collectives, on_device(): lax.all_to_all(sent.reshape(devices, message, 1, LANES), ('gx', 'gy'), sp...  25.6 us
    pallas_call x1, Pallas kernels, on_device(): pl.pallas_call(functools.partial(local_kernel, devices=devices, rows=rows...  5.35 us
    pallas_call x1, Pallas kernels, on_device(): pl.pallas_call(functools.partial(place_kernel, width_x=width_x, width_y=w...  2.25 us

profile of v3, /device:TPU:0, one launch (start us, length us, event | category | flops | bytes accessed | tf_op | source)
XLA Modules:
  0.0 33.2 jit_solution(15363780938627112325)
XLA Ops:
  0.0 5.4 %local.1 = f32[1312,128]{1,0:T(8,128)} custom-call(bf16[256,2048]{1,0:T(8,128)(2,1)} %bitcast.9, s32[16,128]{1,0:T(8,128)} %bitcast.10, f32[16,128]{1,0:T(8,128)} %bitcast.11, f32[16,128]{1,0:T(8,128)} %bitcast.12, s32[8,32]{1,0:T(8,128)} %surf_hbm.1), custom_call_target="tpu_custom_call" | custom-call | tf_op jit(solution)/shard_map/local/pallas_call | solution.py:324
  5.4 25.6 %all_to_all.5 = f32[32,41,1,128]{3,2,1,0:T(1,128)S(1)} all-to-all(f32[32,41,1,128]{3,2,1,0:T(1,128)} %bitcast.8), channel_id=1, replica_groups=mesh['gx'=8,'gy'=4] {'gx','gy'}, dimensions={0} | all-to-all | bytes 1343488 | tf_op jit(solution)/shard_map/all_to_all | solution.py:352
  31.0 2.3 %place.1 = f32[5,4,8,1,8,128]{5,4,3,2,1,0:T(8,128)} custom-call(f32[1312,128]{1,0:T(8,128)S(1)} %bitcast.7), custom_call_target="tpu_custom_call" | custom-call | tf_op jit(solution)/shard_map/place/pallas_call | solution.py:362

commit v4 on v3

--- a/solution.py
+++ b/solution.py
@@ -14,6 +14,7 @@
 RADIX = 4
 WINDOW = 256
 PAIR = 2
+BATCH = 4
 LIMIT = 63 << 20
 NT = (((1,), (1,)), ((), ()))
 
@@ -66,14 +67,14 @@
         copy.start()
     large.start()
 
-    sub = lax.broadcasted_iota(jnp.int32, (8, short), 0)
-    lane = lax.broadcasted_iota(jnp.int32, (8, short), 1)
-    mask = samples - 1
+    sub = lax.broadcasted_iota(jnp.int32, (8, short // 2), 0)
+    lane = 2 * lax.broadcasted_iota(jnp.int32, (8, short // 2), 1) + 1
+    turn = 2 * samples
     bases = [
-        unit_circle(((RADIX * sub + q) * lane) & mask, samples) for q in range(RADIX)
+        unit_circle(((RADIX * sub + q) * lane) & (turn - 1), turn) for q in range(RADIX)
     ]
     for g8 in range(terms // 64):
-        rot_c, rot_s = unit_circle((8 * RADIX * (8 * g8 + sub) * lane) & mask, samples)
+        rot_c, rot_s = unit_circle((8 * RADIX * (8 * g8 + sub) * lane) & (turn - 1), turn)
         for k in range(0, 8, 2):
             for q in range(RADIX):
                 bc, bs = bases[q]
@@ -82,24 +83,36 @@
                     rc, rs = rot_c[t : t + 1], rot_s[t : t + 1]
                     both.append((bc * rc - bs * rs, bs * rc + bc * rs))
                 row = (8 * g8 + k) * 8
-                table[q, row : row + 16, :short] = jnp.concatenate(
+                table[q, row : row + 16, : short // 2] = jnp.concatenate(
                     [both[0][0], both[1][0]], axis=0
                 ).astype(jnp.bfloat16)
-                table[q, row : row + 16, short:] = jnp.concatenate(
+                table[q, row : row + 16, short // 2 :] = jnp.concatenate(
                     [both[0][1], both[1][1]], axis=0
                 ).astype(jnp.bfloat16)
     total[...] = jnp.zeros_like(total)
 
     for copy in small:
         copy.wait()
-    index = idx[...]
+    piece = lax.broadcasted_iota(jnp.int32, idx.shape, 0)
+    back = LANES - 1 - lax.broadcasted_iota(jnp.int32, idx.shape, 1)
+
+    def mirrored(ref):
+        v = ref[...]
+        turned = jnp.take_along_axis(v, back, axis=1, mode="promise_in_bounds")
+        return jnp.where(piece % quarter >= quarter // 2, turned, v)
+
+    index = mirrored(idx)
+    idx[...] = index
     low = jnp.min(index, axis=1, keepdims=True)
     first = jnp.minimum((low // LANES) * LANES, samples - WINDOW)
     high = jnp.max(index, axis=1, keepdims=True) + 2
     longest = jnp.max(high - first)
     steps = (high - first + (LANES - 1)) // LANES
-    cos_phase, sin_phase = circle(phase[...])
-    ws = weight[...]
+    phases = mirrored(phase)
+    phase[...] = phases
+    cos_phase, sin_phase = circle(phases)
+    ws = mirrored(weight)
+    weight[...] = ws
     vs = 1.0 - ws
     near_all = index - first
     large.wait()
@@ -163,29 +176,36 @@
         at = pl.ds(pl.multiple_of(h * LANES + r0, 16), 16)
         top = pl.ds(pl.multiple_of(r0, 16), 16)
         bottom = pl.ds(pl.multiple_of(LANES + r0, 16), 16)
-        for j in range(quarter):
-            re, im = [], []
+        for t in range(quarter // 2):
+            re, im, re_, im_ = [], [], [], []
             for p in range(RADIX):
-                re.append(real[p * quarter + j, at].astype(jnp.float32))
-                im.append(imag[p * quarter + j, at].astype(jnp.float32))
+                re.append(real[p * quarter + t, at].astype(jnp.float32))
+                im.append(imag[p * quarter + t, at].astype(jnp.float32))
+                u = (p + 1) * quarter - 1 - t
+                re_.append(real[u, at].astype(jnp.float32))
+                im_.append(imag[u, at].astype(jnp.float32))
             ar, ai = re[0] + re[2], im[0] + im[2]
             br, bi = re[0] - re[2], im[0] - im[2]
             cr, ci = re[1] + re[3], im[1] + im[3]
             dr, di = re[1] - re[3], im[1] - im[3]
-            folded = [
-                (ar + cr, ai + ci),
-                (br + di, bi - dr),
-                (ar - cr, ai - ci),
-                (br - di, bi + dr),
+            ar_, ai_ = re_[0] + re_[2], im_[0] + im_[2]
+            br_, bi_ = re_[0] - re_[2], im_[0] - im_[2]
+            cr_, ci_ = re_[1] + re_[3], im_[1] + im_[3]
+            er_, di_ = re_[3] - re_[1], im_[1] - im_[3]
+            yz = [
+                (ar + cr, ai + ci, ar_ + cr_, ai_ + ci_, True),
+                (br + di, bi - dr, bi_ + er_, br_ + di_, False),
+                (ar - cr, ai - ci, cr_ - ar_, ci_ - ai_, True),
+                (br - di, bi + dr, er_ - bi_, br_ - di_, True),
             ]
-            left = slice(j * LANES, (j + 1) * LANES)
-            right = slice(short + j * LANES, short + (j + 1) * LANES)
-            for q, (yr, yi) in enumerate(folded):
-                yr, yi = yr.astype(jnp.bfloat16), yi.astype(jnp.bfloat16)
-                fold[h, q, top, left] = yr
-                fold[h, q, top, right] = yi
-                fold[h, q, bottom, left] = yi
-                fold[h, q, bottom, right] = -yr
+            left = slice(t * LANES, (t + 1) * LANES)
+            right = slice(short // 2 + t * LANES, short // 2 + (t + 1) * LANES)
+            for q, (yr, yi, zr, zi, plus) in enumerate(yz):
+                even, odd = (yi + zi, yi - zi) if plus else (yi - zi, yi + zi)
+                fold[h, q, top, left] = (yr + zr).astype(jnp.bfloat16)
+                fold[h, q, top, right] = odd.astype(jnp.bfloat16)
+                fold[h, q, bottom, left] = even.astype(jnp.bfloat16)
+                fold[h, q, bottom, right] = (zr - yr).astype(jnp.bfloat16)
 
     per_half = LANES // surf.shape[1]
 
@@ -263,6 +283,23 @@
     return parts
 
 
+def swap_rows(parts, sub):
+    bit = 1
+    while bit < len(parts):
+        upper = sub & bit != 0
+        mixed = list(parts)
+        for c in range(len(parts)):
+            if c & bit:
+                continue
+            a, b = parts[c], parts[c | bit]
+            both = jnp.where(upper, a, b)
+            mixed[c] = jnp.where(upper, pltpu.roll(both, bit, 0), a)
+            mixed[c | bit] = jnp.where(upper, b, pltpu.roll(both, 8 - bit, 0))
+        parts = mixed
+        bit *= 2
+    return parts
+
+
 def place_kernel(
     in_ref, out_hbm, stage, sem, *, width_x, width_y, rows, message, across, along, scale
 ):
@@ -273,46 +310,38 @@
     sums = in_ref[pl.ds(halves * rows, devices, stride=message), :]
     inverse = 1.0 / (jnp.sum(sums) * scale + 1e-06)
     lane = lax.broadcasted_iota(jnp.int32, (1, LANES), 1)
-    outer, inner = stage.shape[2], stage.shape[4]
-
-    for gx in range(width_x):
-        for group in range(groups):
-            at = gx * groups + group
-            heads = [
-                (gx * width_y + group * chunks + c) * message for c in range(chunks)
-            ]
-            for u in range(outer):
-                if inner == RADIX:
-                    blocks = [pl.ds(head + u, halves * inner, stride=outer) for head in heads]
-                    blocks = [jnp.log(1.0 + in_ref[b, :] * inverse) for b in blocks]
-                    blocks = swap_chunks(blocks, along, lane)
+    sub = lax.broadcasted_iota(jnp.int32, (8, 1), 0)
+    outer, inner = stage.shape[1:3]
+    tiles = width_x * groups
+    for tile in range(tiles):
+        heads = [(tile * chunks + c) * message for c in range(chunks)]
+        for u in range(outer):
+            if inner == RADIX:
+                spans = [pl.ds(head + u, halves * inner, stride=outer) for head in heads]
+                parts = [jnp.log(1.0 + in_ref[span, :] * inverse) for span in spans]
+                parts = swap_rows(swap_chunks(parts, along, lane), sub)
+                for q in range(inner):
+                    stage[tile, u, q] = parts[q]
+            else:
+                for h in range(halves):
+                    spans = [pl.ds(head + h * rows, inner) for head in heads]
+                    parts = [jnp.log(1.0 + in_ref[span, :] * inverse) for span in spans]
+                    parts = swap_chunks(parts, along, lane)
                     for a in range(chunks):
-                        for h in range(halves):
-                            stage[at, a, u, h] = blocks[a][h * inner : (h + 1) * inner]
-                else:
-                    for h in range(halves):
-                        blocks = [pl.ds(head + h * rows + u * inner, inner) for head in heads]
-                        blocks = [jnp.log(1.0 + in_ref[b, :] * inverse) for b in blocks]
-                        blocks = swap_chunks(blocks, along, lane)
-                        for a in range(chunks):
-                            stage[at, a, u, h] = blocks[a]
-            for h in range(halves):
-                for a in range(chunks):
-                    x = gx * across + h * chunks + a
-                    pltpu.make_async_copy(
-                        stage.at[at, a, :, h],
-                        out_hbm.at[:, :, x // 8, group, x % 8],
-                        sem,
-                    ).start()
+                        stage[tile, u, :, h * chunks + a, :] = parts[a]
+        if tile % BATCH == BATCH - 1:
+            for done in range(tile + 1 - BATCH, tile + 1):
+                pltpu.make_async_copy(
+                    stage.at[done],
+                    out_hbm.at[:, :, done // groups, done % groups],
+                    sem,
+                ).start()
     pltpu.make_async_copy(stage, stage, sem).wait()
 
 
-def on_device(spectra, resample_index, resample_weight, disp_phase, surface_block):
+def local_call(spectra, resample_index, resample_weight, disp_phase, surface_block, devices):
     across, along, samples = spectra.shape
     count = across * along
-    width_x = lax.axis_size("gx")
-    width_y = lax.axis_size("gy")
-    devices = width_x * width_y
     rows = KEEP * BLOCK // devices
     halves = count // LANES
     message = halves * rows + 1
@@ -321,13 +350,13 @@
     pieces = samples // LANES
     vmem = pl.BlockSpec(memory_space=pltpu.VMEM)
     hbm = pl.BlockSpec(memory_space=pltpu.HBM)
-    sent = pl.pallas_call(
+    return pl.pallas_call(
         functools.partial(local_kernel, devices=devices, rows=rows, message=message),
         out_shape=jax.ShapeDtypeStruct((devices * message, LANES), jnp.float32),
         in_specs=[hbm] * 5,
         out_specs=vmem,
         scratch_shapes=[
-            pltpu.VMEM((RADIX, terms, 2 * short), jnp.bfloat16),
+            pltpu.VMEM((RADIX, terms, short), jnp.bfloat16),
             pltpu.VMEM((count, samples), jnp.bfloat16),
             pltpu.VMEM((pieces, LANES), jnp.int32),
             pltpu.VMEM((pieces, LANES), jnp.float32),
@@ -335,7 +364,7 @@
             pltpu.VMEM((across, along), jnp.int32),
             pltpu.VMEM((pieces, count, LANES), jnp.bfloat16),
             pltpu.VMEM((pieces, count, LANES), jnp.bfloat16),
-            pltpu.VMEM((halves, RADIX, 2 * LANES, 2 * short), jnp.bfloat16),
+            pltpu.VMEM((halves, RADIX, 2 * LANES, short), jnp.bfloat16),
             pltpu.VMEM((8, LANES), jnp.float32),
             pltpu.SMEM((2 * pieces,), jnp.int32),
             pltpu.SemaphoreType.DMA((5,)),
@@ -349,15 +378,17 @@
         disp_phase.reshape(pieces, LANES),
         surface_block,
     )
-    moved = lax.all_to_all(
-        sent.reshape(devices, message, 1, LANES),
-        ("gx", "gy"),
-        split_axis=0,
-        concat_axis=0,
-        tiled=True,
-    ).reshape(devices * message, LANES)
+
+
+def place_call(moved, rows, width_x, width_y, across, along):
+    devices = width_x * width_y
+    count = across * along
+    halves = count // LANES
+    message = halves * rows + 1
     height, width = width_x * across, width_y * along
     groups = width // LANES
+    vmem = pl.BlockSpec(memory_space=pltpu.VMEM)
+    hbm = pl.BlockSpec(memory_space=pltpu.HBM)
     inner = rows if rows % RADIX else RADIX
     placed = pl.pallas_call(
         functools.partial(
@@ -377,8 +408,7 @@
         out_specs=hbm,
         scratch_shapes=[
             pltpu.VMEM(
-                (width_x * groups, LANES // along, rows // inner, halves, inner, LANES),
-                jnp.float32,
+                (width_x * groups, rows // inner, inner, 8, LANES), jnp.float32
             ),
             pltpu.SemaphoreType.DMA,
         ],
@@ -387,6 +417,25 @@
     )(moved)
     placed = placed.reshape(rows, height // 8, groups, 8, LANES)
     return jnp.transpose(placed, (0, 1, 3, 2, 4)).reshape(rows, height, width)
+
+
+def on_device(spectra, resample_index, resample_weight, disp_phase, surface_block):
+    across, along, samples = spectra.shape
+    width_x = lax.axis_size("gx")
+    width_y = lax.axis_size("gy")
+    devices = width_x * width_y
+    rows = KEEP * BLOCK // devices
+    sent = local_call(
+        spectra, resample_index, resample_weight, disp_phase, surface_block, devices
+    )
+    moved = lax.all_to_all(
+        sent.reshape(devices, -1, 1, LANES),
+        ("gx", "gy"),
+        split_axis=0,
+        concat_axis=0,
+        tiled=True,
+    ).reshape(sent.shape)
+    return place_call(moved, rows, width_x, width_y, across, along)
 
 
 def solution(mesh):

time: 33.5 us -> 31.8 us (0.949)
  Pallas kernels: 7.61 us -> 5.96 us
    pallas_call x2, Pallas kernels: 7.61 us -> 5.96 us  [the longest x1 4.64 us: local_call(): pl.pallas_call(functools.partial(local_kernel, devices=devices, rows=rows...]
where the time goes in v4:
time: 31.8 us; the launch traced here: 31.6 us
  blocking collectives  25.6 us (81%)
  Pallas kernels  5.96 us (19%)
    all_to_all x1, blocking collectives, on_device(): lax.all_to_all(sent.reshape(devices, -1, 1, LANES), ('gx', 'gy'), split_a...  25.6 us
    pallas_call x1, Pallas kernels, local_call(): pl.pallas_call(functools.partial(local_kernel, devices=devices, rows=rows...  4.64 us
    pallas_call x1, Pallas kernels, place_call(): pl.pallas_call(functools.partial(place_kernel, width_x=width_x, width_y=w...  1.32 us

profile of v4, /device:TPU:0, one launch (start us, length us, event | category | flops | bytes accessed | tf_op | source)
XLA Modules:
  0.0 31.6 jit_solution(5080088912732700751)
XLA Ops:
  0.0 4.6 %local.1 = f32[1312,128]{1,0:T(8,128)} custom-call(bf16[256,2048]{1,0:T(8,128)(2,1)} %bitcast.9, s32[16,128]{1,0:T(8,128)} %bitcast.10, f32[16,128]{1,0:T(8,128)} %bitcast.11, f32[16,128]{1,0:T(8,128)} %bitcast.12, s32[8,32]{1,0:T(8,128)} %surf_hbm.1), custom_call_target="tpu_custom_call" | custom-call | tf_op jit(solution)/shard_map/local/pallas_call | solution.py:353
  4.7 25.6 %all_to_all.5 = f32[32,41,1,128]{3,2,1,0:T(1,128)S(1)} all-to-all(f32[32,41,1,128]{3,2,1,0:T(1,128)} %bitcast.8), channel_id=1, replica_groups=mesh['gx'=8,'gy'=4] {'gx','gy'}, dimensions={0} | all-to-all | bytes 1343488 | tf_op jit(solution)/shard_map/all_to_all | solution.py:431
  30.3 1.3 %place.1 = f32[5,4,8,1,8,128]{5,4,3,2,1,0:T(8,128)} custom-call(f32[1312,128]{1,0:T(8,128)S(1)} %bitcast.7), custom_call_target="tpu_custom_call" | custom-call | tf_op jit(solution)/shard_map/place/pallas_call | solution.py:393

commit v5 on v4

--- a/solution.py
+++ b/solution.py
@@ -15,7 +15,8 @@
 WINDOW = 256
 PAIR = 2
 BATCH = 4
-LIMIT = 63 << 20
+LIMIT = 24 << 20
+COST = 2 << 30
 NT = (((1,), (1,)), ((), ()))
 
 
@@ -41,32 +42,9 @@
     return (r % RADIX) * (rows // RADIX) + r // RADIX
 
 
-def local_kernel(
-    spec_hbm, idx_hbm, w_hbm, phase_hbm, surf_hbm, out_ref,
-    table, spec, idx, weight, phase, surf, real, imag, fold, total, starts, sems,
-    *, devices, rows, message,
-):
-    count, samples = spec_hbm.shape
+def table_kernel(table, *, samples):
     short = samples // RADIX
-    depths = samples // 2
-    terms = depths // RADIX
-    per_block = BLOCK // RADIX
-    blocks = depths // BLOCK
-    pieces = samples // LANES
-    quarter = pieces // RADIX
-    halves = count // LANES
-
-    small = [
-        pltpu.make_async_copy(idx_hbm, idx, sems.at[0]),
-        pltpu.make_async_copy(w_hbm, weight, sems.at[1]),
-        pltpu.make_async_copy(phase_hbm, phase, sems.at[2]),
-        pltpu.make_async_copy(surf_hbm, surf, sems.at[3]),
-    ]
-    large = pltpu.make_async_copy(spec_hbm, spec, sems.at[4])
-    for copy in small:
-        copy.start()
-    large.start()
-
+    terms = samples // 2 // RADIX
     sub = lax.broadcasted_iota(jnp.int32, (8, short // 2), 0)
     lane = 2 * lax.broadcasted_iota(jnp.int32, (8, short // 2), 1) + 1
     turn = 2 * samples
@@ -89,10 +67,25 @@
                 table[q, row : row + 16, short // 2 :] = jnp.concatenate(
                     [both[0][1], both[1][1]], axis=0
                 ).astype(jnp.bfloat16)
+
+
+def local_kernel(
+    table, spec, idx_in, w_in, phase_in, surf, out_ref,
+    idx, weight, phase, real, imag, fold, total, starts,
+    *, devices, rows, message,
+):
+    count, samples = spec.shape
+    short = samples // RADIX
+    depths = samples // 2
+    terms = depths // RADIX
+    per_block = BLOCK // RADIX
+    blocks = depths // BLOCK
+    pieces = samples // LANES
+    quarter = pieces // RADIX
+    halves = count // LANES
+
     total[...] = jnp.zeros_like(total)
 
-    for copy in small:
-        copy.wait()
     piece = lax.broadcasted_iota(jnp.int32, idx.shape, 0)
     back = LANES - 1 - lax.broadcasted_iota(jnp.int32, idx.shape, 1)
 
@@ -101,21 +94,20 @@
         turned = jnp.take_along_axis(v, back, axis=1, mode="promise_in_bounds")
         return jnp.where(piece % quarter >= quarter // 2, turned, v)
 
-    index = mirrored(idx)
+    index = mirrored(idx_in)
     idx[...] = index
     low = jnp.min(index, axis=1, keepdims=True)
     first = jnp.minimum((low // LANES) * LANES, samples - WINDOW)
     high = jnp.max(index, axis=1, keepdims=True) + 2
     longest = jnp.max(high - first)
     steps = (high - first + (LANES - 1)) // LANES
-    phases = mirrored(phase)
+    phases = mirrored(phase_in)
     phase[...] = phases
     cos_phase, sin_phase = circle(phases)
-    ws = mirrored(weight)
+    ws = mirrored(w_in)
     weight[...] = ws
     vs = 1.0 - ws
     near_all = index - first
-    large.wait()
 
     source = lax.broadcasted_iota(jnp.int32, (WINDOW, LANES), 0).astype(jnp.bfloat16)
 
@@ -349,29 +341,35 @@
     terms = samples // 2 // RADIX
     pieces = samples // LANES
     vmem = pl.BlockSpec(memory_space=pltpu.VMEM)
-    hbm = pl.BlockSpec(memory_space=pltpu.HBM)
+    table = pl.pallas_call(
+        functools.partial(table_kernel, samples=samples),
+        out_shape=jax.ShapeDtypeStruct((RADIX, terms, short), jnp.bfloat16),
+        out_specs=vmem,
+        cost_estimate=pl.CostEstimate(
+            flops=COST, transcendentals=0, bytes_accessed=2 * RADIX * terms * short
+        ),
+        compiler_params=pltpu.CompilerParams(vmem_limit_bytes=8 << 20),
+        name="table",
+    )()
     return pl.pallas_call(
         functools.partial(local_kernel, devices=devices, rows=rows, message=message),
         out_shape=jax.ShapeDtypeStruct((devices * message, LANES), jnp.float32),
-        in_specs=[hbm] * 5,
+        in_specs=[vmem] * 6,
         out_specs=vmem,
         scratch_shapes=[
-            pltpu.VMEM((RADIX, terms, short), jnp.bfloat16),
-            pltpu.VMEM((count, samples), jnp.bfloat16),
             pltpu.VMEM((pieces, LANES), jnp.int32),
             pltpu.VMEM((pieces, LANES), jnp.float32),
             pltpu.VMEM((pieces, LANES), jnp.float32),
-            pltpu.VMEM((across, along), jnp.int32),
             pltpu.VMEM((pieces, count, LANES), jnp.bfloat16),
             pltpu.VMEM((pieces, count, LANES), jnp.bfloat16),
             pltpu.VMEM((halves, RADIX, 2 * LANES, short), jnp.bfloat16),
             pltpu.VMEM((8, LANES), jnp.float32),
             pltpu.SMEM((2 * pieces,), jnp.int32),
-            pltpu.SemaphoreType.DMA((5,)),
         ],
         compiler_params=pltpu.CompilerParams(vmem_limit_bytes=LIMIT),
         name="local",
     )(
+        table,
         spectra.reshape(count, samples),
         resample_index.reshape(pieces, LANES),
         resample_weight.reshape(pieces, LANES),

time: 31.8 us -> 30.8 us (0.969)
  Pallas kernels: 5.96 us -> 4.35 us
  local copies, waits for them, and re-layouts: 0 us -> 0.85 us
    pallas_call x1, Pallas kernels: 4.64 us -> 2.67 us  [local_call(): pl.pallas_call(functools.partial(local_kernel, devices=devices, rows=rows...]
    unnamed x0 -> x10, local copies, waits for them, and re-layouts: none -> 0.85 us
    pallas_call x0 -> x1, Pallas kernels: none -> 0.37 us  [local_call(): pl.pallas_call(functools.partial(table_kernel, samples=samples), out_shap...]
where the time goes in v5:
time: 30.8 us; the launch traced here: 30.7 us
  blocking collectives  25.4 us (82%)
  Pallas kernels  4.35 us (14%)
  local copies, waits for them, and re-layouts  0.85 us (3%)
    all_to_all x1, blocking collectives, on_device(): lax.all_to_all(sent.reshape(devices, -1, 1, LANES), ('gx', 'gy'), split_a...  25.4 us
    pallas_call x1, Pallas kernels, local_call(): pl.pallas_call(functools.partial(local_kernel, devices=devices, rows=rows...  2.67 us
    pallas_call x1, Pallas kernels, place_call(): pl.pallas_call(functools.partial(place_kernel, width_x=width_x, width_y=w...  1.32 us
    unnamed x10, local copies, waits for them, and re-layouts  0.85 us

profile of v5, /device:TPU:0, one launch (start us, length us, event | category | flops | bytes accessed | tf_op | source)
XLA Modules:
  0.0 30.7 jit_solution(13045722397219808532)
XLA Ops:
  0.0 0.0 copy-start
  0.0 0.0 copy-start.1
  0.0 0.0 copy-start.2
  0.0 0.0 copy-start.3
  0.0 0.4 %table.1 = bf16[4,256,512]{2,1,0:T(8,128)(2,1)S(1)} custom-call(), custom_call_target="tpu_custom_call" | custom-call | flops 2147483648 | bytes 1048576 | tf_op jit(solution)/shard_map/table/pallas_call | solution.py:344
  0.4 0.0 copy-start.4
  0.4 0.8 %copy-done = bf16[8,32,2048]{2,1,0:T(8,128)(2,1)S(1)} copy-done((bf16[8,32,2048]{2,1,0:T(8,128)(2,1)S(1)}, bf16[8,32,2048]{2,1,0:T(8,128)(2,1)}, u32[]{:S(2)}) %copy-start) | copy-done | bytes 1048600
  1.2 0.0 copy-done.1
  1.2 0.0 copy-done.2
  1.2 0.0 copy-done.3
  1.2 0.0 copy-done.4
  1.2 2.7 %local.1 = f32[1312,128]{1,0:T(8,128)S(1)} custom-call(bf16[4,256,512]{2,1,0:T(8,128)(2,1)S(1)} %table.1, bf16[256,2048]{1,0:T(8,128)(2,1)S(1)} %bitcast.9, s32[16,128]{1,0:T(8,128)S(1)} %bitcast.10, f32[16,128]{1,0:T(8,128)S(1)} %bitcast.11, f32[16,128]{1,0:T(8,128)S(1)} %bitcast.12, s32[8,32]{1,0:T(8,128)S(1)} %copy-done.4), custom_call_target="tpu_custom_call" | custom-call | tf_op jit(solution)/shard_map/local/pallas_call | solution.py:354
  3.9 25.4 %all_to_all.5 = f32[32,41,1,128]{3,2,1,0:T(1,128)S(1)} all-to-all(f32[32,41,1,128]{3,2,1,0:T(1,128)S(1)} %bitcast.7), channel_id=1, replica_groups=mesh['gx'=8,'gy'=4] {'gx','gy'}, dimensions={0} | all-to-all | bytes 1343488 | tf_op jit(solution)/shard_map/all_to_all | solution.py:429
  29.3 1.3 %place.1 = f32[5,4,8,1,8,128]{5,4,3,2,1,0:T(8,128)} custom-call(f32[1312,128]{1,0:T(8,128)S(1)} %bitcast.8), custom_call_target="tpu_custom_call" | custom-call | tf_op jit(solution)/shard_map/place/pallas_call | solution.py:391
Async XLA Ops:
  0.0 1.2 %copy-start = (bf16[8,32,2048]{2,1,0:T(8,128)(2,1)S(1)}, bf16[8,32,2048]{2,1,0:T(8,128)(2,1)}, u32[]{:S(2)}) copy-start(bf16[8,32,2048]{2,1,0:T(8,128)(2,1)} %param.5) | copy-start | bytes 3145732
  0.0 1.2 %copy-start.1 = (s32[2048]{0:T(1024)S(1)}, s32[2048]{0:T(1024)}, u32[]{:S(2)}) copy-start(s32[2048]{0:T(1024)} %param.6) | copy-start | bytes 24580
  0.0 1.2 %copy-start.2 = (f32[2048]{0:T(1024)S(1)}, f32[2048]{0:T(1024)}, u32[]{:S(2)}) copy-start(f32[2048]{0:T(1024)} %param.7) | copy-start | bytes 24580
  0.0 1.2 %copy-start.3 = (f32[2048]{0:T(1024)S(1)}, f32[2048]{0:T(1024)}, u32[]{:S(2)}) copy-start(f32[2048]{0:T(1024)} %param.8) | copy-start | bytes 24580
  0.4 0.9 %copy-start.4 = (s32[8,32]{1,0:T(8,128)S(1)}, s32[8,32]{1,0:T(8,128)}, u32[]{:S(2)}) copy-start(s32[8,32]{1,0:T(8,128)} %surf.1) | copy-start | bytes 3076

commit v6 on v5

--- a/solution.py
+++ b/solution.py
@@ -69,9 +69,50 @@
                 ).astype(jnp.bfloat16)
 
 
+def pick(near):
+    source = lax.broadcasted_iota(jnp.int32, (WINDOW, LANES), 0).astype(jnp.bfloat16)
+    hits = []
+    for k in range(2):
+        want = jnp.clip(near + k, -1, WINDOW).astype(jnp.bfloat16)
+        hits.append(jnp.where(source == want, jnp.bfloat16(1), jnp.bfloat16(0)))
+    return jnp.concatenate(hits, axis=1)
+
+
+def finish(pair, w, c, s):
+    r = (1.0 - w) * pair[:, :LANES] + w * pair[:, LANES:]
+    return (r * c).astype(jnp.bfloat16), (r * s).astype(jnp.bfloat16)
+
+
+def plan_kernel(
+    idx_in, w_in, phase_in, picks, idx, weight, cosine, sine, first, spans, *, samples
+):
+    pieces = samples // LANES
+    quarter = pieces // RADIX
+    piece = lax.broadcasted_iota(jnp.int32, idx.shape, 0)
+    back = LANES - 1 - lax.broadcasted_iota(jnp.int32, idx.shape, 1)
+
+    def mirrored(ref):
+        v = ref[...]
+        turned = jnp.take_along_axis(v, back, axis=1, mode="promise_in_bounds")
+        return jnp.where(piece % quarter >= quarter // 2, turned, v)
+
+    index = mirrored(idx_in)
+    idx[...] = index
+    low = jnp.min(index, axis=1, keepdims=True)
+    start = jnp.minimum((low // LANES) * LANES, samples - WINDOW)
+    first[...] = jnp.broadcast_to(start, first.shape)
+    spans[...] = jnp.broadcast_to(
+        jnp.max(index, axis=1, keepdims=True) + 2 - start, spans.shape
+    )
+    weight[...] = mirrored(w_in)
+    cosine[...], sine[...] = circle(mirrored(phase_in))
+    for b in range(pieces):
+        picks[b] = pick(index[b : b + 1] - start[b : b + 1])
+
+
 def local_kernel(
-    table, spec, idx_in, w_in, phase_in, surf, out_ref,
-    idx, weight, phase, real, imag, fold, total, starts,
+    table, spec, picks, idx, weight, cosine, sine, first, spans, surf, out_ref,
+    real, imag, fold, total, starts,
     *, devices, rows, message,
 ):
     count, samples = spec.shape
@@ -86,53 +127,18 @@
 
     total[...] = jnp.zeros_like(total)
 
-    piece = lax.broadcasted_iota(jnp.int32, idx.shape, 0)
-    back = LANES - 1 - lax.broadcasted_iota(jnp.int32, idx.shape, 1)
-
-    def mirrored(ref):
-        v = ref[...]
-        turned = jnp.take_along_axis(v, back, axis=1, mode="promise_in_bounds")
-        return jnp.where(piece % quarter >= quarter // 2, turned, v)
-
-    index = mirrored(idx_in)
-    idx[...] = index
-    low = jnp.min(index, axis=1, keepdims=True)
-    first = jnp.minimum((low // LANES) * LANES, samples - WINDOW)
-    high = jnp.max(index, axis=1, keepdims=True) + 2
-    longest = jnp.max(high - first)
-    steps = (high - first + (LANES - 1)) // LANES
-    phases = mirrored(phase_in)
-    phase[...] = phases
-    cos_phase, sin_phase = circle(phases)
-    ws = mirrored(w_in)
-    weight[...] = ws
-    vs = 1.0 - ws
-    near_all = index - first
-
-    source = lax.broadcasted_iota(jnp.int32, (WINDOW, LANES), 0).astype(jnp.bfloat16)
-
-    def pick(near):
-        hits = []
-        for k in range(2):
-            want = jnp.clip(near + k, -1, WINDOW).astype(jnp.bfloat16)
-            hits.append(jnp.where(source == want, jnp.bfloat16(1), jnp.bfloat16(0)))
-        return jnp.concatenate(hits, axis=1)
-
-    def finish(pair, v, w, c, s):
-        r = v * pair[:, :LANES] + w * pair[:, LANES:]
-        return (r * c).astype(jnp.bfloat16), (r * s).astype(jnp.bfloat16)
-
+    longest = jnp.max(spans[...])
     for b in range(pieces):
-        row = slice(b, b + 1)
+        row = pl.ds(b, 1)
         lines = spec[:, pl.ds(pl.multiple_of(first[b, 0], LANES), WINDOW)]
-        pair = jnp.dot(lines, pick(near_all[row]), preferred_element_type=jnp.float32)
-        real[b], imag[b] = finish(pair, vs[row], ws[row], cos_phase[row], sin_phase[row])
+        pair = jnp.dot(lines, picks[b], preferred_element_type=jnp.float32)
+        real[b], imag[b] = finish(pair, weight[row], cosine[row], sine[row])
 
     @pl.when(longest > WINDOW)
     def _():
         for b in range(pieces):
             starts[b] = first[b, 0]
-            starts[pieces + b] = steps[b, 0]
+            starts[pieces + b] = (spans[b, 0] + (LANES - 1)) // LANES
 
         def redo(b, carry):
             @pl.when(starts[pieces + b] * LANES > WINDOW)
@@ -154,9 +160,8 @@
                     step,
                     jnp.zeros((count, 2 * LANES), jnp.float32),
                 )
-                c, s = circle(phase[pl.ds(b, 1), :])
-                w = weight[pl.ds(b, 1), :]
-                re, im = finish(pair, 1.0 - w, w, c, s)
+                row = pl.ds(b, 1)
+                re, im = finish(pair, weight[row], cosine[row], sine[row])
                 real[b] = re
                 imag[b] = im
 
@@ -351,15 +356,36 @@
         compiler_params=pltpu.CompilerParams(vmem_limit_bytes=8 << 20),
         name="table",
     )()
+    line = lambda dtype: jax.ShapeDtypeStruct((pieces, LANES), dtype)
+    plan = pl.pallas_call(
+        functools.partial(plan_kernel, samples=samples),
+        out_shape=(
+            jax.ShapeDtypeStruct((pieces, WINDOW, 2 * LANES), jnp.bfloat16),
+            line(jnp.int32),
+            line(jnp.float32),
+            line(jnp.float32),
+            line(jnp.float32),
+            line(jnp.int32),
+            line(jnp.int32),
+        ),
+        in_specs=[vmem] * 3,
+        out_specs=(vmem,) * 7,
+        cost_estimate=pl.CostEstimate(
+            flops=1, transcendentals=0, bytes_accessed=1
+        ),
+        compiler_params=pltpu.CompilerParams(vmem_limit_bytes=8 << 20),
+        name="plan",
+    )(
+        resample_index.reshape(pieces, LANES),
+        resample_weight.reshape(pieces, LANES),
+        disp_phase.reshape(pieces, LANES),
+    )
     return pl.pallas_call(
         functools.partial(local_kernel, devices=devices, rows=rows, message=message),
         out_shape=jax.ShapeDtypeStruct((devices * message, LANES), jnp.float32),
-        in_specs=[vmem] * 6,
+        in_specs=[vmem] * 10,
         out_specs=vmem,
         scratch_shapes=[
-            pltpu.VMEM((pieces, LANES), jnp.int32),
-            pltpu.VMEM((pieces, LANES), jnp.float32),
-            pltpu.VMEM((pieces, LANES), jnp.float32),
             pltpu.VMEM((pieces, count, LANES), jnp.bfloat16),
             pltpu.VMEM((pieces, count, LANES), jnp.bfloat16),
             pltpu.VMEM((halves, RADIX, 2 * LANES, short), jnp.bfloat16),
@@ -368,14 +394,7 @@
         ],
         compiler_params=pltpu.CompilerParams(vmem_limit_bytes=LIMIT),
         name="local",
-    )(
-        table,
-        spectra.reshape(count, samples),
-        resample_index.reshape(pieces, LANES),
-        resample_weight.reshape(pieces, LANES),
-        disp_phase.reshape(pieces, LANES),
-        surface_block,
-    )
+    )(table, spectra.reshape(count, samples), *plan, surface_block)
 
 
 def place_call(moved, rows, width_x, width_y, across, along):

time: 30.8 us -> 30.8 us (level)
  local copies, waits for them, and re-layouts: 0.85 us -> 0.42 us
  Pallas kernels: 4.35 us -> 4.7 us
    pallas_call x0 -> x1, Pallas kernels: none -> 0.47 us  [local_call(): pl.pallas_call(functools.partial(plan_kernel, samples=samples), out_shape...]
    unnamed x10, local copies, waits for them, and re-layouts: 0.85 us -> 0.42 us
where the time goes in v6:
time: 30.8 us; the launch traced here: 30.6 us
  blocking collectives  25.4 us (82%)
  Pallas kernels  4.7 us (15%)
  local copies, waits for them, and re-layouts  0.42 us (1%)
    all_to_all x1, blocking collectives, on_device(): lax.all_to_all(sent.reshape(devices, -1, 1, LANES), ('gx', 'gy'), split_a...  25.4 us
    pallas_call x1, Pallas kernels, local_call(): pl.pallas_call(functools.partial(local_kernel, devices=devices, rows=rows...  2.55 us
    pallas_call x1, Pallas kernels, place_call(): pl.pallas_call(functools.partial(place_kernel, width_x=width_x, width_y=w...  1.32 us

profile of v6, /device:TPU:0, one launch (start us, length us, event | category | flops | bytes accessed | tf_op | source)
XLA Modules:
  0.0 30.6 jit_solution(10386617528783604029)
XLA Ops:
  0.0 0.0 copy-start.3
  0.0 0.0 copy-start.2
  0.0 0.0 copy-start.1
  0.0 0.0 copy-start.4
  0.0 0.0 copy-start
  0.0 0.4 %table.1 = bf16[4,256,512]{2,1,0:T(8,128)(2,1)S(1)} custom-call(), custom_call_target="tpu_custom_call" | custom-call | flops 2147483648 | bytes 1048576 | tf_op jit(solution)/shard_map/table/pallas_call | solution.py:349
  0.4 0.3 %copy-done.3 = f32[2048]{0:T(1024)S(1)} copy-done((f32[2048]{0:T(1024)S(1)}, f32[2048]{0:T(1024)}, u32[]{:S(2)}) %copy-start.3) | copy-done | bytes 8216
  0.7 0.0 copy-done.2
  0.7 0.0 copy-done.1
  0.7 0.5 %plan.1 = (bf16[16,256,256]{2,1,0:T(8,128)(2,1)S(1)}, s32[16,128]{1,0:T(8,128)S(1)}, f32[16,128]{1,0:T(8,128)S(1)}, f32[16,128]{1,0:T(8,128)S(1)}, f32[16,128]{1...) custom-call(s32[16,128]{1,0:T(8,128)S(1)} %bitcast.10, f32[16,128]{1,0:T(8,128)S(1)} %bitcast.11, ...), custom_call_target="tpu_custom_call" | custom-call | flops 1 | bytes 1 | tf_op jit(solution)/shard_map/plan/pallas_call | solution.py:360
  1.2 0.0 copy-done.4
  1.2 0.1 copy-done
  1.3 2.5 %local.1 = f32[1312,128]{1,0:T(8,128)S(1)} custom-call(bf16[4,256,512]{2,1,0:T(8,128)(2,1)S(1)} %table.1, bf16[256,2048]{1,0:T(8,128)(2,1)S(1)} %bitcast.9, bf16[16,256,256]{2,1,0:T(8,128)(2,1)S(1)} %get-tuple-element.12.picks, s32[16,128]{1,0:T(8,128)S(1)} %get-tuple-element.13.idx, f32[16,128]{1,0:T(8,128)S(1)} %get-tuple-element.14.weight, ...), custom_call_target="tpu_custom_call" | custom-call | tf_op jit(solution)/shard_map/local/pallas_call | solution.py:383
  3.8 25.4 %all_to_all.5 = f32[32,41,1,128]{3,2,1,0:T(1,128)S(1)} all-to-all(f32[32,41,1,128]{3,2,1,0:T(1,128)S(1)} %bitcast.8), channel_id=1, replica_groups=mesh['gx'=8,'gy'=4] {'gx','gy'}, dimensions={0} | all-to-all | bytes 1343488 | tf_op jit(solution)/shard_map/all_to_all | solution.py:448
  29.3 1.3 %place.1 = f32[5,4,8,1,8,128]{5,4,3,2,1,0:T(8,128)} custom-call(f32[1312,128]{1,0:T(8,128)S(1)} %bitcast.7), custom_call_target="tpu_custom_call" | custom-call | tf_op jit(solution)/shard_map/place/pallas_call | solution.py:410
Async XLA Ops:
  0.0 0.7 %copy-start.3 = (f32[2048]{0:T(1024)S(1)}, f32[2048]{0:T(1024)}, u32[]{:S(2)}) copy-start(f32[2048]{0:T(1024)} %param.8) | copy-start | bytes 24580
  0.0 0.7 %copy-start.2 = (f32[2048]{0:T(1024)S(1)}, f32[2048]{0:T(1024)}, u32[]{:S(2)}) copy-start(f32[2048]{0:T(1024)} %param.7) | copy-start | bytes 24580
  0.0 0.7 %copy-start.1 = (s32[2048]{0:T(1024)S(1)}, s32[2048]{0:T(1024)}, u32[]{:S(2)}) copy-start(s32[2048]{0:T(1024)} %param.6) | copy-start | bytes 24580
  0.0 1.2 %copy-start.4 = (s32[8,32]{1,0:T(8,128)S(1)}, s32[8,32]{1,0:T(8,128)}, u32[]{:S(2)}) copy-start(s32[8,32]{1,0:T(8,128)} %surf.1) | copy-start | bytes 3076
  0.0 1.3 %copy-start = (bf16[8,32,2048]{2,1,0:T(8,128)(2,1)S(1)}, bf16[8,32,2048]{2,1,0:T(8,128)(2,1)}, u32[]{:S(2)}) copy-start(bf16[8,32,2048]{2,1,0:T(8,128)(2,1)} %param.5) | copy-start | bytes 3145732

commit v7 on v6

--- a/solution.py
+++ b/solution.py
@@ -42,7 +42,7 @@
     return (r % RADIX) * (rows // RADIX) + r // RADIX
 
 
-def table_kernel(table, *, samples):
+def make_table(table, samples):
     short = samples // RADIX
     terms = samples // 2 // RADIX
     sub = lax.broadcasted_iota(jnp.int32, (8, short // 2), 0)
@@ -80,12 +80,23 @@
 
 def finish(pair, w, c, s):
     r = (1.0 - w) * pair[:, :LANES] + w * pair[:, LANES:]
-    return (r * c).astype(jnp.bfloat16), (r * s).astype(jnp.bfloat16)
+    rounded = lambda v: v.astype(jnp.bfloat16).astype(jnp.float32)
+    return rounded(r * c), rounded(r * s)
 
 
 def plan_kernel(
-    idx_in, w_in, phase_in, picks, idx, weight, cosine, sine, first, spans, *, samples
+    idx_hbm, w_hbm, phase_hbm, table, picks, idx, weight, cosine, sine, first, spans,
+    idx_in, w_in, phase_in, sems, *, samples,
 ):
+    pairs = ((idx_hbm, idx_in), (w_hbm, w_in), (phase_hbm, phase_in))
+    copies = [
+        pltpu.make_async_copy(a, b, sems.at[i]) for i, (a, b) in enumerate(pairs)
+    ]
+    for copy in copies:
+        copy.start()
+    make_table(table, samples)
+    for copy in copies:
+        copy.wait()
     pieces = samples // LANES
     quarter = pieces // RADIX
     piece = lax.broadcasted_iota(jnp.int32, idx.shape, 0)
@@ -176,11 +187,11 @@
         for t in range(quarter // 2):
             re, im, re_, im_ = [], [], [], []
             for p in range(RADIX):
-                re.append(real[p * quarter + t, at].astype(jnp.float32))
-                im.append(imag[p * quarter + t, at].astype(jnp.float32))
+                re.append(real[p * quarter + t, at])
+                im.append(imag[p * quarter + t, at])
                 u = (p + 1) * quarter - 1 - t
-                re_.append(real[u, at].astype(jnp.float32))
-                im_.append(imag[u, at].astype(jnp.float32))
+                re_.append(real[u, at])
+                im_.append(imag[u, at])
             ar, ai = re[0] + re[2], im[0] + im[2]
             br, bi = re[0] - re[2], im[0] - im[2]
             cr, ci = re[1] + re[3], im[1] + im[3]
@@ -234,23 +245,13 @@
                 out_ref[places[m] : places[m] + stop - m, :] = kept[m:stop]
                 m = stop
 
-    @pl.loop(0, LANES // 32)
-    def _(chunk):
-        for part in range(2):
-            fold_lines(0, chunk * 32 + part * 16)
-
     for h in range(halves):
-        for q0 in range(0, RADIX, PAIR):
-
-            @pl.when(longest > 0)
-            def _():
-                for q in range(q0, q0 + PAIR):
-                    transform(h, q)
-                if h + 1 < halves:
-                    share = LANES * PAIR // RADIX
-                    begin = q0 // PAIR * share
-                    for r0 in range(begin, begin + share, 16):
-                        fold_lines(h + 1, r0)
+        for r0 in range(0, LANES, 16):
+            fold_lines(h, r0)
+
+    for h in range(halves):
+        for q in range(RADIX):
+            transform(h, q)
 
     partial = jnp.sum(total[...], axis=0, keepdims=True)
     for dest in range(devices):
@@ -345,21 +346,13 @@
     short = samples // RADIX
     terms = samples // 2 // RADIX
     pieces = samples // LANES
+    hbm = pl.BlockSpec(memory_space=pltpu.HBM)
     vmem = pl.BlockSpec(memory_space=pltpu.VMEM)
-    table = pl.pallas_call(
-        functools.partial(table_kernel, samples=samples),
-        out_shape=jax.ShapeDtypeStruct((RADIX, terms, short), jnp.bfloat16),
-        out_specs=vmem,
-        cost_estimate=pl.CostEstimate(
-            flops=COST, transcendentals=0, bytes_accessed=2 * RADIX * terms * short
-        ),
-        compiler_params=pltpu.CompilerParams(vmem_limit_bytes=8 << 20),
-        name="table",
-    )()
     line = lambda dtype: jax.ShapeDtypeStruct((pieces, LANES), dtype)
     plan = pl.pallas_call(
         functools.partial(plan_kernel, samples=samples),
         out_shape=(
+            jax.ShapeDtypeStruct((RADIX, terms, short), jnp.bfloat16),
             jax.ShapeDtypeStruct((pieces, WINDOW, 2 * LANES), jnp.bfloat16),
             line(jnp.int32),
             line(jnp.float32),
@@ -368,17 +361,24 @@
             line(jnp.int32),
             line(jnp.int32),
         ),
-        in_specs=[vmem] * 3,
-        out_specs=(vmem,) * 7,
+        in_specs=[hbm] * 3,
+        out_specs=(vmem,) * 8,
+        scratch_shapes=[
+            pltpu.VMEM((pieces, LANES), jnp.int32),
+            pltpu.VMEM((pieces, LANES), jnp.float32),
+            pltpu.VMEM((pieces, LANES), jnp.float32),
+            pltpu.SemaphoreType.DMA((3,)),
+        ],
         cost_estimate=pl.CostEstimate(
-            flops=1, transcendentals=0, bytes_accessed=1
+            flops=COST, transcendentals=0, bytes_accessed=6 * RADIX * terms * short
         ),
         compiler_params=pltpu.CompilerParams(vmem_limit_bytes=8 << 20),
         name="plan",
     )(
-        resample_index.reshape(pieces, LANES),
-        resample_weight.reshape(pieces, LANES),
-        disp_phase.reshape(pieces, LANES),
+        *(
+            pltpu.with_memory_space_constraint(v.reshape(pieces, LANES), pltpu.HBM)
+            for v in (resample_index, resample_weight, disp_phase)
+        )
     )
     return pl.pallas_call(
         functools.partial(local_kernel, devices=devices, rows=rows, message=message),
@@ -386,15 +386,15 @@
         in_specs=[vmem] * 10,
         out_specs=vmem,
         scratch_shapes=[
-            pltpu.VMEM((pieces, count, LANES), jnp.bfloat16),
-            pltpu.VMEM((pieces, count, LANES), jnp.bfloat16),
+            pltpu.VMEM((pieces, count, LANES), jnp.float32),
+            pltpu.VMEM((pieces, count, LANES), jnp.float32),
             pltpu.VMEM((halves, RADIX, 2 * LANES, short), jnp.bfloat16),
             pltpu.VMEM((8, LANES), jnp.float32),
             pltpu.SMEM((2 * pieces,), jnp.int32),
         ],
         compiler_params=pltpu.CompilerParams(vmem_limit_bytes=LIMIT),
         name="local",
-    )(table, spectra.reshape(count, samples), *plan, surface_block)
+    )(plan[0], spectra.reshape(count, samples), *plan[1:], surface_block)
 
 
 def place_call(moved, rows, width_x, width_y, across, along):

time: 30.8 us -> 30.9 us (level)
  Pallas kernels: 4.7 us -> 5.18 us
  local copies, waits for them, and re-layouts: 0.42 us -> 0.01 us
    pallas_call x1, Pallas kernels: 0.47 us -> 1.32 us  [local_call(): pl.pallas_call(functools.partial(plan_kernel, samples=samples), out_shape...]
    unnamed x10 -> x4, local copies, waits for them, and re-layouts: 0.42 us -> 0.01 us
    pallas_call x1 -> x0, Pallas kernels: 0.37 us -> none  [local_call(): pl.pallas_call(functools.partial(table_kernel, samples=samples), out_shap...]
where the time goes in v7:
time: 30.9 us; the launch traced here: 30.6 us
  blocking collectives  25.4 us (82%)
  Pallas kernels  5.18 us (17%)
    all_to_all x1, blocking collectives, on_device(): lax.all_to_all(sent.reshape(devices, -1, 1, LANES), ('gx', 'gy'), split_a...  25.4 us
    pallas_call x1, Pallas kernels, local_call(): pl.pallas_call(functools.partial(local_kernel, devices=devices, rows=rows...  2.55 us
    pallas_call x1, Pallas kernels, local_call(): pl.pallas_call(functools.partial(plan_kernel, samples=samples), out_shape...  1.32 us
    pallas_call x1, Pallas kernels, place_call(): pl.pallas_call(functools.partial(place_kernel, width_x=width_x, width_y=w...  1.32 us

profile of v7, /device:TPU:0, one launch (start us, length us, event | category | flops | bytes accessed | tf_op | source)
XLA Modules:
  0.0 30.6 jit_solution(10880540837010898110)
XLA Ops:
  0.0 0.0 copy-start
  0.0 0.0 copy-start.1
  0.0 1.3 %plan.1 = (bf16[4,256,512]{2,1,0:T(8,128)(2,1)S(1)}, bf16[16,256,256]{2,1,0:T(8,128)(2,1)S(1)}, s32[16,128]{1,0:T(8,128)S(1)}, f32[16,128]{1,0:T(8,128)S(1)}, f3...) custom-call(s32[16,128]{1,0:T(8,128)} %bitcast.10, ...), custom_call_target="tpu_custom_call" | custom-call | flops 2147483648 | bytes 3145728 | tf_op jit(solution)/shard_map/plan/pallas_call | solution.py:352
  1.3 0.0 copy-done
  1.3 0.0 copy-done.1
  1.3 2.5 %local.1 = f32[1312,128]{1,0:T(8,128)S(1)} custom-call(bf16[4,256,512]{2,1,0:T(8,128)(2,1)S(1)} %get-tuple-element.13.table, bf16[256,2048]{1,0:T(8,128)(2,1)S(1)} %bitcast.9, bf16[16,256,256]{2,1,0:T(8,128)(2,1)S(1)} %get-tuple-element.14.picks, s32[16,128]{1,0:T(8,128)S(1)} %get-tuple-element.15.idx, f32[16,128]{1,0:T(8,128)S(1)} %get-tuple-element.16.weight, ...), custom_call_target="tpu_custom_call" | custom-call | tf_op jit(solution)/shard_map/local/pallas_call | solution.py:383
  3.9 25.4 %all_to_all.5 = f32[32,41,1,128]{3,2,1,0:T(1,128)S(1)} all-to-all(f32[32,41,1,128]{3,2,1,0:T(1,128)S(1)} %bitcast.8), channel_id=1, replica_groups=mesh['gx'=8,'gy'=4] {'gx','gy'}, dimensions={0} | all-to-all | bytes 1343488 | tf_op jit(solution)/shard_map/all_to_all | solution.py:448
  29.3 1.3 %place.1 = f32[5,4,8,1,8,128]{5,4,3,2,1,0:T(8,128)} custom-call(f32[1312,128]{1,0:T(8,128)S(1)} %bitcast.7), custom_call_target="tpu_custom_call" | custom-call | tf_op jit(solution)/shard_map/place/pallas_call | solution.py:410
Async XLA Ops:
  0.0 1.3 %copy-start = (bf16[8,32,2048]{2,1,0:T(8,128)(2,1)S(1)}, bf16[8,32,2048]{2,1,0:T(8,128)(2,1)}, u32[]{:S(2)}) copy-start(bf16[8,32,2048]{2,1,0:T(8,128)(2,1)} %param.5) | copy-start | bytes 3145732
  0.0 1.3 %copy-start.1 = (s32[8,32]{1,0:T(8,128)S(1)}, s32[8,32]{1,0:T(8,128)}, u32[]{:S(2)}) copy-start(s32[8,32]{1,0:T(8,128)} %surf.1) | copy-start | bytes 3076

commit v8 on v4

--- a/solution.py
+++ b/solution.py
@@ -13,9 +13,9 @@
 LANES = 128
 RADIX = 4
 WINDOW = 256
-PAIR = 2
 BATCH = 4
-LIMIT = 63 << 20
+PAD = 8
+LIMIT = 24 << 20
 NT = (((1,), (1,)), ((), ()))
 
 
@@ -43,7 +43,7 @@
 
 def local_kernel(
     spec_hbm, idx_hbm, w_hbm, phase_hbm, surf_hbm, out_ref,
-    table, spec, idx, weight, phase, surf, real, imag, fold, total, starts, sems,
+    table, spec, picks, idx, weight, phase, surf, real, imag, fold, total, starts, sems,
     *, devices, rows, message,
 ):
     count, samples = spec_hbm.shape
@@ -113,9 +113,7 @@
     cos_phase, sin_phase = circle(phases)
     ws = mirrored(weight)
     weight[...] = ws
-    vs = 1.0 - ws
     near_all = index - first
-    large.wait()
 
     source = lax.broadcasted_iota(jnp.int32, (WINDOW, LANES), 0).astype(jnp.bfloat16)
 
@@ -124,17 +122,24 @@
         for k in range(2):
             want = jnp.clip(near + k, -1, WINDOW).astype(jnp.bfloat16)
             hits.append(jnp.where(source == want, jnp.bfloat16(1), jnp.bfloat16(0)))
-        return jnp.concatenate(hits, axis=1)
-
-    def finish(pair, v, w, c, s):
-        r = v * pair[:, :LANES] + w * pair[:, LANES:]
-        return (r * c).astype(jnp.bfloat16), (r * s).astype(jnp.bfloat16)
-
+        return hits
+
+    def finish(left, right, w, c, s):
+        r = (1.0 - w) * left + w * right
+        rounded = lambda v: v.astype(jnp.bfloat16).astype(jnp.float32)
+        return rounded(r * c), rounded(r * s)
+
+    for b in range(pieces):
+        near = near_all[b : b + 1]
+        picks[b, :, :LANES], picks[b, :, LANES:] = pick(near)
+    large.wait()
     for b in range(pieces):
         row = slice(b, b + 1)
         lines = spec[:, pl.ds(pl.multiple_of(first[b, 0], LANES), WINDOW)]
-        pair = jnp.dot(lines, pick(near_all[row]), preferred_element_type=jnp.float32)
-        real[b], imag[b] = finish(pair, vs[row], ws[row], cos_phase[row], sin_phase[row])
+        pair = jnp.dot(lines, picks[b], preferred_element_type=jnp.float32)
+        real[b, :count], imag[b, :count] = finish(
+            pair[:, :LANES], pair[:, LANES:], ws[row], cos_phase[row], sin_phase[row]
+        )
 
     @pl.when(longest > WINDOW)
     def _():
@@ -149,7 +154,7 @@
 
                 def step(i, pair):
                     k = pl.multiple_of(starts[b] + i * LANES, LANES)
-                    hits = pick(near - k)[:LANES]
+                    hits = jnp.concatenate(pick(near - k), axis=1)[:LANES]
                     return pair + jnp.dot(
                         spec[:, pl.ds(k, LANES)],
                         hits,
@@ -164,9 +169,9 @@
                 )
                 c, s = circle(phase[pl.ds(b, 1), :])
                 w = weight[pl.ds(b, 1), :]
-                re, im = finish(pair, 1.0 - w, w, c, s)
-                real[b] = re
-                imag[b] = im
+                re, im = finish(pair[:, :LANES], pair[:, LANES:], w, c, s)
+                real[b, pl.ds(0, count)] = re
+                imag[b, pl.ds(0, count)] = im
 
             return carry
 
@@ -179,11 +184,11 @@
         for t in range(quarter // 2):
             re, im, re_, im_ = [], [], [], []
             for p in range(RADIX):
-                re.append(real[p * quarter + t, at].astype(jnp.float32))
-                im.append(imag[p * quarter + t, at].astype(jnp.float32))
+                re.append(real[p * quarter + t, at])
+                im.append(imag[p * quarter + t, at])
                 u = (p + 1) * quarter - 1 - t
-                re_.append(real[u, at].astype(jnp.float32))
-                im_.append(imag[u, at].astype(jnp.float32))
+                re_.append(real[u, at])
+                im_.append(imag[u, at])
             ar, ai = re[0] + re[2], im[0] + im[2]
             br, bi = re[0] - re[2], im[0] - im[2]
             cr, ci = re[1] + re[3], im[1] + im[3]
@@ -214,7 +219,7 @@
         surface = jnp.concatenate([surf[x : x + 1, :] for x in lines_at], axis=1)
         chosen = [surface == s for s in range(1, blocks - KEEP + 1)]
         depth = lax.dot_general(
-            table[q], fold[h, q], NT, preferred_element_type=jnp.float32
+            table[q], fold[h, q, : 2 * LANES], NT, preferred_element_type=jnp.float32
         )
         re, im = depth[:, :LANES], depth[:, LANES:]
         power = re * re + im * im
@@ -237,23 +242,11 @@
                 out_ref[places[m] : places[m] + stop - m, :] = kept[m:stop]
                 m = stop
 
-    @pl.loop(0, LANES // 32)
-    def _(chunk):
-        for part in range(2):
-            fold_lines(0, chunk * 32 + part * 16)
-
     for h in range(halves):
-        for q0 in range(0, RADIX, PAIR):
-
-            @pl.when(longest > 0)
-            def _():
-                for q in range(q0, q0 + PAIR):
-                    transform(h, q)
-                if h + 1 < halves:
-                    share = LANES * PAIR // RADIX
-                    begin = q0 // PAIR * share
-                    for r0 in range(begin, begin + share, 16):
-                        fold_lines(h + 1, r0)
+        for r0 in range(0, LANES, 16):
+            fold_lines(h, r0)
+        for q in range(RADIX):
+            transform(h, q)
 
     partial = jnp.sum(total[...], axis=0, keepdims=True)
     for dest in range(devices):
@@ -358,13 +351,14 @@
         scratch_shapes=[
             pltpu.VMEM((RADIX, terms, short), jnp.bfloat16),
             pltpu.VMEM((count, samples), jnp.bfloat16),
+            pltpu.VMEM((pieces, WINDOW, 2 * LANES), jnp.bfloat16),
             pltpu.VMEM((pieces, LANES), jnp.int32),
             pltpu.VMEM((pieces, LANES), jnp.float32),
             pltpu.VMEM((pieces, LANES), jnp.float32),
             pltpu.VMEM((across, along), jnp.int32),
-            pltpu.VMEM((pieces, count, LANES), jnp.bfloat16),
-            pltpu.VMEM((pieces, count, LANES), jnp.bfloat16),
-            pltpu.VMEM((halves, RADIX, 2 * LANES, short), jnp.bfloat16),
+            pltpu.VMEM((pieces, count + PAD, LANES), jnp.float32),
+            pltpu.VMEM((pieces, count + PAD, LANES), jnp.float32),
+            pltpu.VMEM((halves, RADIX, 2 * LANES + 2 * PAD, short), jnp.bfloat16),
             pltpu.VMEM((8, LANES), jnp.float32),
             pltpu.SMEM((2 * pieces,), jnp.int32),
             pltpu.SemaphoreType.DMA((5,)),
@@ -372,11 +366,16 @@
         compiler_params=pltpu.CompilerParams(vmem_limit_bytes=LIMIT),
         name="local",
     )(
-        spectra.reshape(count, samples),
-        resample_index.reshape(pieces, LANES),
-        resample_weight.reshape(pieces, LANES),
-        disp_phase.reshape(pieces, LANES),
-        surface_block,
+        *(
+            pltpu.with_memory_space_constraint(v, pltpu.HBM)
+            for v in (
+                spectra.reshape(count, samples),
+                resample_index.reshape(pieces, LANES),
+                resample_weight.reshape(pieces, LANES),
+                disp_phase.reshape(pieces, LANES),
+                surface_block,
+            )
+        ),
     )
 
 

time: 31.8 us -> 30.6 us (0.962)
  Pallas kernels: 5.96 us -> 5 us
    pallas_call x1, Pallas kernels: 4.64 us -> 3.68 us  [local_call(): pl.pallas_call(functools.partial(local_kernel, devices=devices, rows=rows...]
where the time goes in v8:
time: 30.6 us; the launch traced here: 30.4 us
  blocking collectives  25.4 us (83%)
  Pallas kernels  5 us (16%)
    all_to_all x1, blocking collectives, on_device(): lax.all_to_all(sent.reshape(devices, -1, 1, LANES), ('gx', 'gy'), split_a...  25.4 us
    pallas_call x1, Pallas kernels, local_call(): pl.pallas_call(functools.partial(local_kernel, devices=devices, rows=rows...  3.68 us
    pallas_call x1, Pallas kernels, place_call(): pl.pallas_call(functools.partial(place_kernel, width_x=width_x, width_y=w...  1.32 us

profile of v8, /device:TPU:0, one launch (start us, length us, event | category | flops | bytes accessed | tf_op | source)
XLA Modules:
  0.0 30.4 jit_solution(15737688968229350871)
XLA Ops:
  0.0 3.7 %local.1 = f32[1312,128]{1,0:T(8,128)S(1)} custom-call(bf16[256,2048]{1,0:T(8,128)(2,1)} %bitcast.9, s32[16,128]{1,0:T(8,128)} %bitcast.10, f32[16,128]{1,0:T(8,128)} %bitcast.11, f32[16,128]{1,0:T(8,128)} %bitcast.12, s32[8,32]{1,0:T(8,128)} %surf_hbm.1), custom_call_target="tpu_custom_call" | custom-call | tf_op jit(solution)/shard_map/local/pallas_call | solution.py:346
  3.7 25.4 %all_to_all.5 = f32[32,41,1,128]{3,2,1,0:T(1,128)S(1)} all-to-all(f32[32,41,1,128]{3,2,1,0:T(1,128)S(1)} %bitcast.8), channel_id=1, replica_groups=mesh['gx'=8,'gy'=4] {'gx','gy'}, dimensions={0} | all-to-all | bytes 1343488 | tf_op jit(solution)/shard_map/all_to_all | solution.py:430
  29.1 1.3 %place.1 = f32[5,4,8,1,8,128]{5,4,3,2,1,0:T(8,128)} custom-call(f32[1312,128]{1,0:T(8,128)S(1)} %bitcast.7), custom_call_target="tpu_custom_call" | custom-call | tf_op jit(solution)/shard_map/place/pallas_call | solution.py:392

commit v9 on v8

--- a/solution.py
+++ b/solution.py
@@ -13,7 +13,7 @@
 LANES = 128
 RADIX = 4
 WINDOW = 256
-BATCH = 4
+BATCH = 1
 PAD = 8
 LIMIT = 24 << 20
 NT = (((1,), (1,)), ((), ()))

time: 30.6 us -> 30.6 us (level)
  no operation moved by 1% of the time
where the time goes in v9:
time: 30.6 us; the launch traced here: 30.4 us
  blocking collectives  25.4 us (83%)
  Pallas kernels  4.95 us (16%)
    all_to_all x1, blocking collectives, on_device(): lax.all_to_all(sent.reshape(devices, -1, 1, LANES), ('gx', 'gy'), split_a...  25.4 us
    pallas_call x1, Pallas kernels, local_call(): pl.pallas_call(functools.partial(local_kernel, devices=devices, rows=rows...  3.68 us
    pallas_call x1, Pallas kernels, place_call(): pl.pallas_call(functools.partial(place_kernel, width_x=width_x, width_y=w...  1.27 us

profile of v9, /device:TPU:0, one launch (start us, length us, event | category | flops | bytes accessed | tf_op | source)
XLA Modules:
  0.0 30.4 jit_solution(8689749029827112154)
XLA Ops:
  0.0 3.7 %local.1 = f32[1312,128]{1,0:T(8,128)S(1)} custom-call(bf16[256,2048]{1,0:T(8,128)(2,1)} %bitcast.9, s32[16,128]{1,0:T(8,128)} %bitcast.10, f32[16,128]{1,0:T(8,128)} %bitcast.11, f32[16,128]{1,0:T(8,128)} %bitcast.12, s32[8,32]{1,0:T(8,128)} %surf_hbm.1), custom_call_target="tpu_custom_call" | custom-call | tf_op jit(solution)/shard_map/local/pallas_call | solution.py:346
  3.7 25.4 %all_to_all.5 = f32[32,41,1,128]{3,2,1,0:T(1,128)S(1)} all-to-all(f32[32,41,1,128]{3,2,1,0:T(1,128)S(1)} %bitcast.8), channel_id=1, replica_groups=mesh['gx'=8,'gy'=4] {'gx','gy'}, dimensions={0} | all-to-all | bytes 1343488 | tf_op jit(solution)/shard_map/all_to_all | solution.py:430
  29.1 1.3 %place.1 = f32[5,4,8,1,8,128]{5,4,3,2,1,0:T(8,128)} custom-call(f32[1312,128]{1,0:T(8,128)S(1)} %bitcast.7), custom_call_target="tpu_custom_call" | custom-call | tf_op jit(solution)/shard_map/place/pallas_call | solution.py:392

commit v10 on v8

--- a/solution.py
+++ b/solution.py
@@ -131,12 +131,12 @@
 
     for b in range(pieces):
         near = near_all[b : b + 1]
-        picks[b, :, :LANES], picks[b, :, LANES:] = pick(near)
+        picks[b, :WINDOW, :LANES], picks[b, :WINDOW, LANES:] = pick(near)
     large.wait()
     for b in range(pieces):
         row = slice(b, b + 1)
         lines = spec[:, pl.ds(pl.multiple_of(first[b, 0], LANES), WINDOW)]
-        pair = jnp.dot(lines, picks[b], preferred_element_type=jnp.float32)
+        pair = jnp.dot(lines, picks[b, :WINDOW], preferred_element_type=jnp.float32)
         real[b, :count], imag[b, :count] = finish(
             pair[:, :LANES], pair[:, LANES:], ws[row], cos_phase[row], sin_phase[row]
         )
@@ -219,7 +219,7 @@
         surface = jnp.concatenate([surf[x : x + 1, :] for x in lines_at], axis=1)
         chosen = [surface == s for s in range(1, blocks - KEEP + 1)]
         depth = lax.dot_general(
-            table[q], fold[h, q, : 2 * LANES], NT, preferred_element_type=jnp.float32
+            table[q, :terms], fold[h, q, : 2 * LANES], NT, preferred_element_type=jnp.float32
         )
         re, im = depth[:, :LANES], depth[:, LANES:]
         power = re * re + im * im
@@ -349,9 +349,9 @@
         in_specs=[hbm] * 5,
         out_specs=vmem,
         scratch_shapes=[
-            pltpu.VMEM((RADIX, terms, short), jnp.bfloat16),
+            pltpu.VMEM((RADIX, terms + 2 * PAD, short), jnp.bfloat16),
             pltpu.VMEM((count, samples), jnp.bfloat16),
-            pltpu.VMEM((pieces, WINDOW, 2 * LANES), jnp.bfloat16),
+            pltpu.VMEM((pieces, WINDOW + 2 * PAD, 2 * LANES), jnp.bfloat16),
             pltpu.VMEM((pieces, LANES), jnp.int32),
             pltpu.VMEM((pieces, LANES), jnp.float32),
             pltpu.VMEM((pieces, LANES), jnp.float32),

time: 30.6 us -> 30.6 us (level)
  no operation moved by 1% of the time
where the time goes in v10:
time: 30.6 us; the launch traced here: 30.4 us
  blocking collectives  25.4 us (83%)
  Pallas kernels  5 us (16%)
    all_to_all x1, blocking collectives, on_device(): lax.all_to_all(sent.reshape(devices, -1, 1, LANES), ('gx', 'gy'), split_a...  25.4 us
    pallas_call x1, Pallas kernels, local_call(): pl.pallas_call(functools.partial(local_kernel, devices=devices, rows=rows...  3.68 us
    pallas_call x1, Pallas kernels, place_call(): pl.pallas_call(functools.partial(place_kernel, width_x=width_x, width_y=w...  1.32 us

profile of v10, /device:TPU:0, one launch (start us, length us, event | category | flops | bytes accessed | tf_op | source)
XLA Modules:
  0.0 30.4 jit_solution(15915298956969081742)
XLA Ops:
  0.0 3.7 %local.1 = f32[1312,128]{1,0:T(8,128)S(1)} custom-call(bf16[256,2048]{1,0:T(8,128)(2,1)} %bitcast.9, s32[16,128]{1,0:T(8,128)} %bitcast.10, f32[16,128]{1,0:T(8,128)} %bitcast.11, f32[16,128]{1,0:T(8,128)} %bitcast.12, s32[8,32]{1,0:T(8,128)} %surf_hbm.1), custom_call_target="tpu_custom_call" | custom-call | tf_op jit(solution)/shard_map/local/pallas_call | solution.py:346
  3.7 25.4 %all_to_all.5 = f32[32,41,1,128]{3,2,1,0:T(1,128)S(1)} all-to-all(f32[32,41,1,128]{3,2,1,0:T(1,128)S(1)} %bitcast.8), channel_id=1, replica_groups=mesh['gx'=8,'gy'=4] {'gx','gy'}, dimensions={0} | all-to-all | bytes 1343488 | tf_op jit(solution)/shard_map/all_to_all | solution.py:430
  29.1 1.3 %place.1 = f32[5,4,8,1,8,128]{5,4,3,2,1,0:T(8,128)} custom-call(f32[1312,128]{1,0:T(8,128)S(1)} %bitcast.7), custom_call_target="tpu_custom_call" | custom-call | tf_op jit(solution)/shard_map/place/pallas_call | solution.py:392

commit v11 on v10

--- a/solution.py
+++ b/solution.py
@@ -13,8 +13,8 @@
 LANES = 128
 RADIX = 4
 WINDOW = 256
-BATCH = 4
-PAD = 8
+BATCH = 2
+PAD = 24
 LIMIT = 24 << 20
 NT = (((1,), (1,)), ((), ()))
 

time: 30.6 us -> 30.6 us (level)
  no operation moved by 1% of the time
where the time goes in v11:
time: 30.6 us; the launch traced here: 30.4 us
  blocking collectives  25.4 us (83%)
  Pallas kernels  4.97 us (16%)
    all_to_all x1, blocking collectives, on_device(): lax.all_to_all(sent.reshape(devices, -1, 1, LANES), ('gx', 'gy'), split_a...  25.4 us
    pallas_call x1, Pallas kernels, local_call(): pl.pallas_call(functools.partial(local_kernel, devices=devices, rows=rows...  3.68 us
    pallas_call x1, Pallas kernels, place_call(): pl.pallas_call(functools.partial(place_kernel, width_x=width_x, width_y=w...  1.28 us

profile of v11, /device:TPU:0, one launch (start us, length us, event | category | flops | bytes accessed | tf_op | source)
XLA Modules:
  0.0 30.4 jit_solution(161151455657767317)
XLA Ops:
  0.0 3.7 %local.1 = f32[1312,128]{1,0:T(8,128)S(1)} custom-call(bf16[256,2048]{1,0:T(8,128)(2,1)} %bitcast.9, s32[16,128]{1,0:T(8,128)} %bitcast.10, f32[16,128]{1,0:T(8,128)} %bitcast.11, f32[16,128]{1,0:T(8,128)} %bitcast.12, s32[8,32]{1,0:T(8,128)} %surf_hbm.1), custom_call_target="tpu_custom_call" | custom-call | tf_op jit(solution)/shard_map/local/pallas_call | solution.py:346
  3.7 25.4 %all_to_all.5 = f32[32,41,1,128]{3,2,1,0:T(1,128)S(1)} all-to-all(f32[32,41,1,128]{3,2,1,0:T(1,128)S(1)} %bitcast.8), channel_id=1, replica_groups=mesh['gx'=8,'gy'=4] {'gx','gy'}, dimensions={0} | all-to-all | bytes 1343488 | tf_op jit(solution)/shard_map/all_to_all | solution.py:430
  29.1 1.3 %place.1 = f32[5,4,8,1,8,128]{5,4,3,2,1,0:T(8,128)} custom-call(f32[1312,128]{1,0:T(8,128)S(1)} %bitcast.7), custom_call_target="tpu_custom_call" | custom-call | tf_op jit(solution)/shard_map/place/pallas_call | solution.py:392
